TPU v7x, 128 devices: a whole 4x4x4 slice. The times are simulated.
128 devices in a mesh: req: 32 (over z, x, core), tp: 4 (over y).
Axes of the slice: x: 4, y: 4, z: 4, core: 2. Of those that a mesh axis runs over, the one named last changes fastest.
Arguments:
- tokens: bfloat16 [16384, 2048], P('req', 'tp'), may hold values from -6 to 6
- first_gain: float32 [2048], replicated, may hold values from 0.5 to 1.5
- first_shift: float32 [2048], replicated, may hold values from -2.5 to 2.5
- project_weight: bfloat16 [2048, 3, 2048], P(None, None, 'tp'), may hold values from -0.125 to 0.125
- project_bias: float32 [3, 2048], P(None, 'tp'), may hold values from -3 to 3
- output_weight: bfloat16 [2048, 2048], P('tp'), may hold values from -0.125 to 0.125
- second_gain: float32 [2048], replicated, may hold values from 0.5 to 1.5
- second_shift: float32 [2048], replicated, may hold values from -2.5 to 2.5
- expand_weight: bfloat16 [2048, 2, 3072], P(None, None, 'tp'), may hold values from -0.125 to 0.125
- contract_weight: bfloat16 [3072, 2048], P('tp'), may hold values from -0.109375 to 0.109375
- prior_cache: bfloat16 [32, 1024, 2, 2048], P('req', None, None, 'tp'), may hold values from -21 to 21
- prior_len: int32 [32], replicated, may hold values from 16 to 1024, as said below
- slot_map: int32 [32], replicated, may hold values from 0 to 31, each once
- block_table: int32 [32, 6], replicated, may hold values from 0 to 11, as said below
Outputs:
- mixed_out: bfloat16 [16384, 2048], P('req', 'tp')
- page_pool: bfloat16 [32, 12, 256, 2, 1024], P('req', None, None, None, 'tp')
Inputs may be any that keep to these rules, and one draw needn't show every extreme that they name: `prior_len`: every request has at least 16 cached positions; some request has exactly 1024. `block_table`: rows 2g and 2g+1 together name each of the 12 pages exactly once.
All inputs are finite; a program needn't handle non-finite values.
Results may differ from a plain program's by a relative error of at most 0.018.
Values may be sent and summed in bfloat16 or wider, within the bound.
No kernel may reach another device: no remote copies, remote signals or barrier semaphores. Data moves between devices by JAX's collectives and lax.ppermute only.
A program may use at most 128 MiB of HBM per device.

v0:
```python
import jax
import jax.numpy as jnp
from jax import lax
from jax.experimental import pallas as pl
from jax.experimental.pallas import tpu as pltpu
from jax.sharding import PartitionSpec as P


HEAD_DIM = 64
ROTARY = 16
BLOCK = 256
EPSILON = 1e-05
ROPE_BASE = 10000.0
MASK_FILL = -1e30
BF = jnp.bfloat16
F32 = jnp.float32


OFFSETS = (0, 3, 1, 2)


def shift_by(value, step):
    return lax.ppermute(value, "tp", [(i, (i + step) % 4) for i in range(4)])


def ring_gather(top, bottom):
    left_top = shift_by(top, 1)
    right_bottom = shift_by(bottom, -1)
    left_bottom = shift_by(bottom, 1)
    right_top = shift_by(top, -1)
    far_top = shift_by(left_top, 1)
    far_bottom = shift_by(right_bottom, -1)
    return (top, bottom, left_top, left_bottom, right_top, right_bottom, far_top, far_bottom)


def ring_scatter(parts):
    own_top, own_bottom, left_top, left_bottom, right_top, right_bottom, far_top, far_bottom = parts
    add = lambda a, b: (a.astype(F32) + b.astype(F32))
    far_top = shift_by(far_top, 1)
    far_bottom = shift_by(far_bottom, -1)
    from_left_bottom = shift_by(right_bottom, 1)
    from_right_top = shift_by(left_top, -1)
    from_left_top = shift_by(add(right_top, far_top).astype(BF), 1)
    from_right_bottom = shift_by(add(left_bottom, far_bottom).astype(BF), -1)
    top = add(own_top, from_right_top) + from_left_top.astype(F32)
    bottom = add(own_bottom, from_left_bottom) + from_right_bottom.astype(F32)
    return top, bottom


def norm_into(normed, pieces, gain, shift, blocks, half):
    width = pieces[0].shape[1]
    total = 4 * width
    step = 64
    for part in range(2):
        refs = pieces[part::2]

        def body(index, carry, refs=refs, part=part):
            at = pl.multiple_of(index * step, step)
            rows = [ref[pl.ds(at, step), :].astype(F32) for ref in refs]
            mean = sum(jnp.sum(row, axis=1, keepdims=True) for row in rows) / total
            rows = [row - mean for row in rows]
            spread = sum(jnp.sum(row * row, axis=1, keepdims=True) for row in rows) / total
            scale = lax.rsqrt(spread + EPSILON)
            for slot, row in enumerate(rows):
                line = blocks[slot]
                value = row * scale * gain[pl.ds(line, 1), :] + shift[pl.ds(line, 1), :]
                normed[pl.ds(part * half + at, step), slot * width : (slot + 1) * width] = value.astype(BF)
            return carry

        lax.fori_loop(0, half // step, body, 0)


def project_kernel(
    o0, o1, l0, l1, r0, r1, f0, f1, gain, shift, weight, bias, cosine, sine_a, sine_b, queries, keys, values, buffer, normed, sems
):
    device = lax.axis_index("tp")
    width = o0.shape[1]
    half = o0.shape[0]
    blocks = [lax.rem(device + offset, 4) for offset in OFFSETS]
    copies = []
    for slot in range(4):
        copies.append(
            pltpu.make_async_copy(
                weight.at[:, pl.ds(blocks[slot] * width, width), :],
                buffer.at[:, pl.ds(slot * width, width), :],
                sems.at[slot],
            )
        )
        copies[-1].start()
    norm_into(normed, (o0, o1, l0, l1, r0, r1, f0, f1), gain, shift, blocks, half)
    for copy in copies:
        copy.wait()
    outs = (queries, keys, values)
    for part in range(2):
        rows = slice(part * half, (part + 1) * half)
        for which in range(3):
            product = jnp.dot(normed[rows, :], buffer[which], preferred_element_type=F32)
            product = product + bias[which : which + 1, :]
            if which == 2:
                outs[which][rows, :] = product.astype(BF)
                continue
            for tile in range(width // 128):
                lanes = slice(tile * 128, (tile + 1) * 128)
                value = product[:, lanes]
                up = pltpu.roll(value, 128 - ROTARY // 2, 1)
                down = pltpu.roll(value, ROTARY // 2, 1)
                turned = value * cosine[rows, :] + up * sine_a[rows, :] + down * sine_b[rows, :]
                if which == 0:
                    turned = turned * HEAD_DIM ** (-0.5)
                outs[which][rows, lanes] = turned.astype(BF)


VMEM = pltpu.MemorySpace.VMEM
SMEM = pltpu.MemorySpace.SMEM


def specs(*kinds):
    table = {"v": pl.BlockSpec(memory_space=VMEM), "s": pl.BlockSpec(memory_space=SMEM), "a": pl.BlockSpec(memory_space=pl.ANY)}
    return [table[kind] for kind in kinds]


PARAMS = pltpu.CompilerParams(vmem_limit_bytes=56 * 1024 * 1024)


def project(pieces, gain, shift, weight, bias, tables):
    half, width = pieces[0].shape
    out = jax.ShapeDtypeStruct((2 * half, width), BF)
    return pl.pallas_call(
        project_kernel,
        out_shape=(out, out, out),
        in_specs=specs(*"v" * 8, "v", "v", "a", "v", "v", "v", "v"),
        out_specs=tuple(specs("v", "v", "v")),
        scratch_shapes=[
            pltpu.VMEM((3, 4 * width, width), BF),
            pltpu.VMEM((2 * half, 4 * width), BF),
            pltpu.SemaphoreType.DMA((4,)),
        ],
        compiler_params=PARAMS,
        name="project",
    )(*pieces, gain, shift, weight, bias, *tables)


def attend_kernel(lengths, queries, new_keys, new_values, old_keys, old_values, weight, *refs):
    outs, (buffer, mixed, sems) = refs[:8], refs[8:]
    device = lax.axis_index("tp")
    prior = lengths[lax.axis_index("req")]
    rows_all, width = queries.shape
    cached = old_keys.shape[0]
    blocks = [lax.rem(device + offset, 4) for offset in OFFSETS]
    copies = []
    for slot in range(4):
        copies.append(
            pltpu.make_async_copy(
                weight.at[:, pl.ds(blocks[slot] * width, width)], buffer.at[:, slot * width : (slot + 1) * width], sems.at[slot]
            )
        )
        copies[-1].start()
    step = 256
    contract = (((1,), (1,)), ((), ()))
    for part in range(rows_all // step):
        rows = slice(part * step, (part + 1) * step)
        seen = (part + 1) * step

        def body(pair, carry, rows=rows, seen=seen, part=part):
            lanes = pl.ds(pl.multiple_of(pair * 128, 128), 128)
            query = queries[rows, lanes]
            old_key, new_key = old_keys[:, lanes], new_keys[:seen, lanes]
            old_value, new_value = old_values[:, lanes], new_values[:seen, lanes]
            lane = lax.broadcasted_iota(jnp.int32, (step, 128), 1)
            old_allowed = lax.broadcasted_iota(jnp.int32, (1, cached), 1) < prior
            new_allowed = lax.broadcasted_iota(jnp.int32, (step, seen), 1) <= lax.broadcasted_iota(
                jnp.int32, (step, seen), 0
            ) + part * step
            results = []
            for head in range(2):
                own = (lane < HEAD_DIM) if head == 0 else (lane >= HEAD_DIM)
                masked = jnp.where(own, query, jnp.zeros((), BF))
                old_score = lax.dot_general(masked, old_key, contract, preferred_element_type=F32)
                old_score = jnp.where(old_allowed, old_score, MASK_FILL)
                new_score = lax.dot_general(masked, new_key, contract, preferred_element_type=F32)
                new_score = jnp.where(new_allowed, new_score, MASK_FILL)
                highest = jnp.maximum(
                    jnp.max(old_score, axis=1, keepdims=True), jnp.max(new_score, axis=1, keepdims=True)
                )
                old_weight = jnp.exp(old_score - highest)
                new_weight = jnp.exp(new_score - highest)
                total = jnp.sum(old_weight, axis=1, keepdims=True) + jnp.sum(new_weight, axis=1, keepdims=True)
                value = jnp.dot(old_weight.astype(BF), old_value, preferred_element_type=F32) + jnp.dot(
                    new_weight.astype(BF), new_value, preferred_element_type=F32
                )
                results.append(value / total)
            mixed[rows, lanes] = jnp.where(lane < HEAD_DIM, results[0], results[1]).astype(BF)
            return carry

        lax.fori_loop(0, width // 128, body, 0)
    for copy in copies:
        copy.wait()
    for part in range(rows_all // step):
        rows = slice(part * step, (part + 1) * step)
        for slot in range(4):
            product = jnp.dot(mixed[rows, :], buffer[:, slot * width : (slot + 1) * width], preferred_element_type=F32)
            outs[2 * slot + part][...] = product.astype(BF)


def attend(lengths, queries, new_keys, new_values, old_keys, old_values, weight):
    rows, width = queries.shape
    return pl.pallas_call(
        attend_kernel,
        out_shape=(jax.ShapeDtypeStruct((rows // 2, width), BF),) * 8,
        in_specs=specs("s", "v", "v", "v", "v", "v", "a"),
        out_specs=tuple(specs(*"v" * 8)),
        scratch_shapes=[pltpu.VMEM((width, 4 * width), BF), pltpu.VMEM((rows, width), BF), pltpu.SemaphoreType.DMA((4,))],
        compiler_params=PARAMS,
        name="attend",
    )(lengths, queries, new_keys, new_values, old_keys, old_values, weight)


def forward_kernel(o0, o1, l0, l1, r0, r1, f0, f1, gain, shift, expand, contract, *refs):
    outs, (expand_buffer, contract_buffer, normed, sems) = refs[:8], refs[8:]
    device = lax.axis_index("tp")
    half, width = o0.shape
    blocks = [lax.rem(device + offset, 4) for offset in OFFSETS]
    copies = []
    for slot in range(4):
        copies.append(
            pltpu.make_async_copy(
                expand.at[:, pl.ds(blocks[slot] * width, width), :],
                expand_buffer.at[:, slot * width : (slot + 1) * width, :],
                sems.at[0, slot],
            )
        )
    for slot in range(4):
        copies.append(
            pltpu.make_async_copy(
                contract.at[:, pl.ds(blocks[slot] * width, width)],
                contract_buffer.at[:, slot * width : (slot + 1) * width],
                sems.at[1, slot],
            )
        )
    for copy in copies:
        copy.start()
    norm_into(normed, (o0, o1, l0, l1, r0, r1, f0, f1), gain, shift, blocks, half)
    for copy in copies:
        copy.wait()
    for part in range(2):
        rows = slice(part * half, (part + 1) * half)
        gate = jnp.dot(normed[rows, :], expand_buffer[0], preferred_element_type=F32)
        up = jnp.dot(normed[rows, :], expand_buffer[1], preferred_element_type=F32)
        hidden = (gate / (1.0 + jnp.exp(-gate)) * up).astype(BF)
        for slot in range(4):
            product = jnp.dot(hidden, contract_buffer[:, slot * width : (slot + 1) * width], preferred_element_type=F32)
            outs[2 * slot + part][...] = product.astype(BF)


def feed_forward(pieces, gain, shift, expand, contract):
    half, width = pieces[0].shape
    hidden = expand.shape[2]
    return pl.pallas_call(
        forward_kernel,
        out_shape=(jax.ShapeDtypeStruct((half, width), BF),) * 8,
        in_specs=specs(*"v" * 8, "v", "v", "a", "a"),
        out_specs=tuple(specs(*"v" * 8)),
        scratch_shapes=[
            pltpu.VMEM((2, 4 * width, hidden), BF),
            pltpu.VMEM((hidden, 4 * width), BF),
            pltpu.VMEM((2 * half, 4 * width), BF),
            pltpu.SemaphoreType.DMA((2, 4)),
        ],
        compiler_params=PARAMS,
        name="feed_forward",
    )(*pieces, gain, shift, expand, contract)


def split_kernel(cache, keys, values):
    _, _, width = cache.shape
    step = 128
    row = lax.broadcasted_iota(jnp.int32, (2 * step, 2 * step), 0)
    column = lax.broadcasted_iota(jnp.int32, (2 * step, 2 * step), 1)
    source = jnp.where(row < step, 2 * row, 2 * (row - step) + 1)
    chosen = jnp.where(column == source, 1.0, 0.0).astype(BF)

    def body(index, carry):
        at = pl.multiple_of(index * step, step)
        pair = cache[pl.ds(at, step)].reshape(2 * step, width)
        parted = jnp.dot(chosen, pair, preferred_element_type=F32).astype(BF)
        keys[pl.ds(at, step), :] = parted[:step]
        values[pl.ds(at, step), :] = parted[step:]
        return carry

    lax.fori_loop(0, cache.shape[0] // step, body, 0)


def split(cache):
    rows, _, width = cache.shape
    out = jax.ShapeDtypeStruct((rows, width), BF)
    return pl.pallas_call(
        split_kernel,
        out_shape=(out, out),
        in_specs=specs("v"),
        out_specs=tuple(specs("v", "v")),
        compiler_params=PARAMS,
        name="split",
    )(cache)


def find_owners(slot_map, owners):
    def body(index, carry):
        owners[slot_map[index]] = index
        return carry

    lax.fori_loop(0, slot_map.shape[0], body, 0)


def mix_kernel(slot_map, pieces, keys, values, out, owners, stage, sems):
    count, rows, _, width = pieces.shape
    half = width // 2
    fresh = keys.shape[0] // count
    find_owners(slot_map, owners)

    def send(slot, carry):
        group = slot // 2
        for side in range(2):
            pltpu.make_async_copy(
                pieces.at[owners[slot], :, :, side * half : (side + 1) * half],
                out.at[2 * group + side, pl.ds((slot - 2 * group) * rows, rows)],
                sems.at[0],
            ).start()
        return carry

    lax.fori_loop(0, count, send, 0)

    def weave(slot, carry):
        at = pl.multiple_of(slot * fresh, fresh)
        for side in range(2):
            lanes = slice(side * half, (side + 1) * half)
            stage[slot, side * fresh : (side + 1) * fresh, 0, :] = keys[pl.ds(at, fresh), lanes]
            stage[slot, side * fresh : (side + 1) * fresh, 1, :] = values[pl.ds(at, fresh), lanes]
        return carry

    lax.fori_loop(0, count, weave, 0)
    last = pltpu.make_async_copy(stage, out.at[:, 2 * rows :], sems.at[1])
    last.start()
    first = out.at[:, : 2 * rows]
    pltpu.make_async_copy(first, first, sems.at[0]).wait()
    last.wait()


def mix(slot_map, pieces, keys, values):
    count, rows, _, width = pieces.shape
    fresh = keys.shape[0] // count
    return pl.pallas_call(
        mix_kernel,
        out_shape=jax.ShapeDtypeStruct((count, 2 * rows + 2 * fresh, 2, width // 2), BF),
        in_specs=specs("s", "v", "v", "v"),
        out_specs=specs("a")[0],
        scratch_shapes=[
            pltpu.SMEM((count,), jnp.int32),
            pltpu.VMEM((count, 2 * fresh, 2, width // 2), BF),
            pltpu.SemaphoreType.DMA((2,)),
        ],
        compiler_params=PARAMS,
        name="mix",
    )(slot_map, pieces, keys, values)


def reorder_kernel(slot_map, mixed, out, owners, sem):
    count, rows, _, _ = mixed.shape
    fresh = out.shape[2]
    find_owners(slot_map, owners)

    def send(slot, carry):
        group = slot // 2
        for side in range(2):
            pltpu.make_async_copy(
                mixed.at[owners[slot], pl.ds(rows - (2 - side) * fresh, fresh)],
                out.at[2 * group + side, slot - 2 * group],
                sem,
            ).start()
        return carry

    lax.fori_loop(0, count, send, 0)
    pltpu.make_async_copy(out, out, sem).wait()


def reorder(slot_map, mixed, fresh):
    count, _, _, width = mixed.shape
    return pl.pallas_call(
        reorder_kernel,
        out_shape=jax.ShapeDtypeStruct((count, 2, fresh, 2, width), BF),
        in_specs=specs("s", "a"),
        out_specs=specs("v")[0],
        scratch_shapes=[pltpu.SMEM((count,), jnp.int32), pltpu.SemaphoreType.DMA],
        compiler_params=PARAMS,
        name="reorder",
    )(slot_map, mixed)


def pages_kernel(slot_map, prior_len, table, mixed, new, out, owners, full, blank, sems):
    count, _, new_rows, _, _ = new.shape
    old_rows = (mixed.shape[1] - 2 * new_rows) // 2
    cached, fresh = count * old_rows, count * new_rows
    blocks = (cached + fresh) // BLOCK
    group = lax.axis_index("req") // 2
    find_owners(slot_map, owners)
    for slot in range(2):

        def load(index, carry, slot=slot):
            pltpu.make_async_copy(
                mixed.at[index, pl.ds(slot * old_rows, old_rows)], full.at[slot, pl.ds(index * old_rows, old_rows)], sems.at[0, slot]
            ).start()
            return carry

        lax.fori_loop(0, count, load, 0)
    blank[...] = jnp.zeros(blank.shape, BF)
    for slot in range(2):
        whole = full.at[slot, pl.ds(0, cached)]
        pltpu.make_async_copy(whole, whole, sems.at[0, slot]).wait()
        length = prior_len[owners[2 * group + slot]]

        def fill(index, carry, slot=slot, length=length):
            pltpu.make_async_copy(
                blank, full.at[slot, pl.ds(length + fresh + index * BLOCK, BLOCK)], sems.at[1, slot]
            ).start()
            return carry

        lax.fori_loop(0, cached // BLOCK, fill, 0)

        def store(index, carry, slot=slot, length=length):
            pltpu.make_async_copy(
                new.at[index, slot], full.at[slot, pl.ds(length + index * new_rows, new_rows)], sems.at[1, slot]
            ).start()
            return carry

        lax.fori_loop(0, count, store, 0)
    for slot in range(2):
        whole = full.at[slot, pl.ds(0, cached + fresh)]
        pltpu.make_async_copy(whole, whole, sems.at[1, slot]).wait()
        for block in range(blocks):
            pltpu.make_async_copy(
                full.at[slot, pl.ds(block * BLOCK, BLOCK)],
                out.at[0, table[(2 * group + slot) * blocks + block]],
                sems.at[2, 0],
            ).start()
    pltpu.make_async_copy(out, out, sems.at[2, 0]).wait()


def pages(slot_map, prior_len, table, mixed, new):
    count, _, new_rows, _, width = new.shape
    cached = count * (mixed.shape[1] - 2 * new_rows) // 2
    fresh = count * new_rows
    return pl.pallas_call(
        pages_kernel,
        out_shape=jax.ShapeDtypeStruct((1, 2 * (cached + fresh) // BLOCK, BLOCK, 2, width), BF),
        in_specs=specs("s", "s", "s", "a", "a"),
        out_specs=specs("a")[0],
        scratch_shapes=[
            pltpu.SMEM((count,), jnp.int32),
            pltpu.VMEM((2, 2 * cached + fresh, 2, width), BF),
            pltpu.VMEM((BLOCK, 2, width), BF),
            pltpu.SemaphoreType.DMA((3, 2)),
        ],
        compiler_params=PARAMS,
        name="pages",
    )(slot_map, prior_len, table, mixed, new)


def rotary_tables(prior_count, rows):
    lane = jnp.arange(128, dtype=jnp.int32) % HEAD_DIM
    half_rot = ROTARY // 2
    frequency = ROPE_BASE ** (-2.0 * (lane % half_rot).astype(F32) / ROTARY)
    frequency = jnp.where(lane < ROTARY, frequency, 0.0)
    positions = (prior_count + jnp.arange(rows, dtype=jnp.int32)).astype(F32)
    angles = positions[:, None] * frequency[None, :]
    sine = jnp.sin(angles)
    return (
        jnp.cos(angles),
        jnp.where(lane < half_rot, -sine, 0.0),
        jnp.where((lane >= half_rot) & (lane < ROTARY), sine, 0.0),
    )


def exchange(pieces):
    return lax.all_to_all(pieces, "req", split_axis=0, concat_axis=0, tiled=True)


def layer(
    tokens,
    first_gain,
    first_shift,
    project_weight,
    project_bias,
    output_weight,
    second_gain,
    second_shift,
    expand_weight,
    contract_weight,
    prior_cache,
    prior_len,
    slot_map,
    block_table,
):
    count = slot_map.shape[0]
    rows, width = tokens.shape
    half = rows // 2
    cached = prior_cache.shape[1]
    prior_count = prior_len[lax.axis_index("req")]
    top, bottom = tokens[:half], tokens[half:]
    pieces = ring_gather(top, bottom)
    old = exchange(prior_cache.reshape(count, cached // count, 2, width))
    old_keys, old_values = split(prior_cache[0])
    tables = rotary_tables(prior_count, rows)
    queries, new_keys, new_values = project(
        pieces,
        first_gain.reshape(4, width),
        first_shift.reshape(4, width),
        jnp.transpose(project_weight, (1, 0, 2)),
        project_bias,
        tables,
    )
    parts = attend(prior_len, queries, new_keys, new_values, old_keys, old_values, output_weight)
    mixed = mix(slot_map, old, new_keys, new_values)
    mixed = exchange(mixed)
    top_sum, bottom_sum = ring_scatter(parts)
    top = (top.astype(F32) + top_sum).astype(BF)
    bottom = (bottom.astype(F32) + bottom_sum).astype(BF)
    pieces = ring_gather(top, bottom)
    parts = feed_forward(
        pieces,
        second_gain.reshape(4, width),
        second_shift.reshape(4, width),
        jnp.transpose(expand_weight, (1, 0, 2)),
        contract_weight,
    )
    new = reorder(slot_map, mixed, rows // count)
    new = exchange(new)
    top_sum, bottom_sum = ring_scatter(parts)
    result = jnp.concatenate(
        [(top.astype(F32) + top_sum).astype(BF), (bottom.astype(F32) + bottom_sum).astype(BF)], axis=0
    )
    page_pool = pages(slot_map, prior_len, block_table.reshape(-1), mixed, new)
    return (result, page_pool)


def solution(mesh):
    return jax.shard_map(
        layer,
        mesh=mesh,
        in_specs=(
            P("req", "tp"),
            P(),
            P(),
            P(None, None, "tp"),
            P(None, "tp"),
            P("tp", None),
            P(),
            P(),
            P(None, None, "tp"),
            P("tp", None),
            P("req", None, None, "tp"),
            P(),
            P(),
            P(),
        ),
        out_specs=(P("req", "tp"), P("req", None, None, None, "tp")),
        check_vma=False,
    )
```

profile of v0, /device:TPU:0, one launch (start us, length us, event | category | flops | bytes accessed | tf_op | source)
XLA Modules:
  0.0 170.2 jit_solution(16644931367077819542)
XLA Ops:
  0.7 8.4 %all-to-all-start = ((bf16[32,32,2,512]{3,2,1,0:T(2,128)(2,1)}), bf16[32,32,2,512]{3,2,1,0:T(2,128)(2,1)S(1)}, u32[]{:S(2)}, u32[]{:S(2)}) async-start(bf16[32,32,2,512]{3,2,1,0:T(2,128)(2,1)} %bitcast.8), calls=%async_computation | async-start | bytes 4194304 | tf_op jit(solution)/shard_map/all_to_all | solution.py:483
  12.8 2.9 %collective-permute-start.2 = (bf16[256,512]{1,0:T(8,128)(2,1)S(1)}, bf16[256,512]{1,0:T(8,128)(2,1)}, u32[]{:S(2)}, u32[]{:S(2)}) collective-permute-start(bf16[256,512]{1,0:T(8,128)(2,1)S(1)} %get-tuple-element.47.o0), channel_id=1, source_target_pairs={{0,3},{1,0},{2,1},{3,2},{4,7},{5,4},{6,5},{7,6},{8,11},{9,8},{10,9... | collective-permute-start | bytes 786440 | tf_op jit(solution)/shard_map/ppermute | solution.py:23
  17.0 2.7 %collective-permute-done.l0 = bf16[256,512]{1,0:T(8,128)(2,1)S(1)} collective-permute-done((bf16[256,512]{1,0:T(8,128)(2,1)S(1)}, bf16[256,512]{1,0:T(8,128)(2,1)S(1)}, u32[]{:S(2)}, u32[]{:S(2)}) %collective-permute-start) | collective-permute-done | bytes 262176 | tf_op jit(solution)/shard_map/ppermute | solution.py:23
  20.0 2.9 %collective-permute-start.5 = (bf16[256,512]{1,0:T(8,128)(2,1)S(1)}, bf16[256,512]{1,0:T(8,128)(2,1)}, u32[]{:S(2)}, u32[]{:S(2)}) collective-permute-start(bf16[256,512]{1,0:T(8,128)(2,1)S(1)} %collective-permute-done.3.r1), channel_id=1, source_target_pairs={{0,3},{1,0},{2,1},{3,2},{4,7},{5,4},{6,5},{7,6},{8,11},{9,8},{10,9... | collective-permute-start | bytes 786440 | tf_op jit(solution)/shard_map/ppermute | solution.py:23
  24.1 1.9 %fusion = (f32[512,128]{1,0:T(8,128)}, f32[512,128]{1,0:T(8,128)}, f32[512,128]{1,0:T(8,128)}) fusion(f32[128]{0:T(128)S(1)} %compare_select_fusion.2, f32[512]{0:T(512)S(1)} %add_convert_fusion.8, pred[128]{0:T(512)(128)(4,1)S(1)} %get-tuple-element.51, pred[128]{0:T(512)(128)(4,1)S(1)} %get-tuple-element.52), kind=kLoop, calls=%fused_computation.12 | loop fusion | flops 262144 | bytes 789248 | tf_op jit(solution)/shard_map/jit(_where)/select_n | solution.py:478
  26.0 4.4 %collective-permute-done.4.f0 = bf16[256,512]{1,0:T(8,128)(2,1)} collective-permute-done((bf16[256,512]{1,0:T(8,128)(2,1)S(1)}, bf16[256,512]{1,0:T(8,128)(2,1)}, u32[]{:S(2)}, u32[]{:S(2)}) %collective-permute-start.4) | collective-permute-done | bytes 262176 | tf_op jit(solution)/shard_map/ppermute | solution.py:23
  30.4 8.8 %project.1 = (bf16[512,512]{1,0:T(8,128)(2,1)}, bf16[512,512]{1,0:T(8,128)(2,1)}, bf16[512,512]{1,0:T(8,128)(2,1)}) custom-call(bf16[256,512]{1,0:T(8,128)(2,1)} %copy-done.8, bf16[256,512]{1,0:T(8,128)(2,1)} %copy-done.7, bf16[256,512]{1,0:T(8,128)(2,1)} %copy-done.11, bf16[256,512]{1,0:T(8,128)(2,1)} %copy-done.13, ...), custom_call_target="tpu_custom_call" | custom-call | tf_op jit(solution)/shard_map/project/pallas_call | solution.py:128
  40.6 5.0 %mix.1 = bf16[32,96,2,256]{3,2,1,0:T(2,128)(2,1)} custom-call(s32[32]{0:T(128)} %slot_map.5, bf16[32,32,2,512]{3,2,1,0:T(2,128)(2,1)} %copy-done.1, bf16[512,512]{1,0:T(8,128)(2,1)} %get-tuple-element.24.new_keys.keys, bf16[512,512]{1,0:T(8,128)(2,1)} %get-tuple-element.25.new_values.values), custom_call_target="tpu_custom_call" | custom-call | tf_op jit(solution)/shard_map/mix/pallas_call | solution.py:351
  45.6 7.2 %all-to-all-start.1 = ((bf16[32,96,2,256]{3,2,1,0:T(2,128)(2,1)}), bf16[32,96,2,256]{3,2,1,0:T(2,128)(2,1)S(1)}, u32[]{:S(2)}, u32[]{:S(2)}) async-start(bf16[32,96,2,256]{3,2,1,0:T(2,128)(2,1)} %mix.1), calls=%async_computation.1 | async-start | bytes 6291456 | tf_op jit(solution)/shard_map/all_to_all | solution.py:483
  52.9 4.8 %split.1 = (bf16[1024,512]{1,0:T(8,128)(2,1)}, bf16[1024,512]{1,0:T(8,128)(2,1)}) custom-call(bf16[1024,2,512]{2,1,0:T(2,128)(2,1)} %bitcast.9), custom_call_target="tpu_custom_call" | custom-call | tf_op jit(solution)/shard_map/split/pallas_call | solution.py:296
  57.7 16.1 %attend.1 = (bf16[256,512]{1,0:T(8,128)(2,1)}, bf16[256,512]{1,0:T(8,128)(2,1)}, bf16[256,512]{1,0:T(8,128)(2,1)}, bf16[256,512]{1,0:T(8,128)(2,1)}, bf16[256,51...) custom-call(s32[32]{0:T(128)} %prior_len.1, ...), custom_call_target="tpu_custom_call" | custom-call | tf_op jit(solution)/shard_map/attend/pallas_call | solution.py:207
  73.8 3.1 %collective-permute-start.10 = (bf16[256,512]{1,0:T(8,128)(2,1)}, bf16[256,512]{1,0:T(8,128)(2,1)S(1)}, u32[]{:S(2)}, u32[]{:S(2)}) collective-permute-start(bf16[256,512]{1,0:T(8,128)(2,1)} %get-tuple-element.35), channel_id=1, source_target_pairs={{0,3},{1,0},{2,1},{3,2},{4,7},{5,4},{6,5},{7,6},{8,11},{9,8},{10,9... | collective-permute-start | bytes 786440 | tf_op jit(solution)/shard_map/ppermute | solution.py:23
  77.5 2.7 %collective-permute-start.6 = (bf16[256,512]{1,0:T(8,128)(2,1)}, bf16[256,512]{1,0:T(8,128)(2,1)S(1)}, u32[]{:S(2)}, u32[]{:S(2)}) collective-permute-start(bf16[256,512]{1,0:T(8,128)(2,1)} %get-tuple-element.29), channel_id=1, source_target_pairs={{0,3},{1,0},{2,1},{3,2},{4,7},{5,4},{6,5},{7,6},{8,11},{9,8},{10,9... | collective-permute-start | bytes 786440 | tf_op jit(solution)/shard_map/ppermute | solution.py:23
  80.2 3.8 %collective-permute-done.10 = bf16[256,512]{1,0:T(8,128)(2,1)S(1)} collective-permute-done((bf16[256,512]{1,0:T(8,128)(2,1)}, bf16[256,512]{1,0:T(8,128)(2,1)S(1)}, u32[]{:S(2)}, u32[]{:S(2)}) %collective-permute-start.10) | collective-permute-done | bytes 262176 | tf_op jit(solution)/shard_map/ppermute | solution.py:23
  84.9 3.7 %collective-permute-start.11 = (bf16[256,512]{1,0:T(8,128)(2,1)S(1)}, bf16[256,512]{1,0:T(8,128)(2,1)S(1)}, u32[]{:S(2)}, u32[]{:S(2)}) collective-permute-start(bf16[256,512]{1,0:T(8,128)(2,1)S(1)} %add_convert_fusion.5), channel_id=1, source_target_pairs={{0,3},{1,0},{2,1},{3,2},{4,7},{5,4},{6,5},{7,6},{8,11},{9,8},{10,9... | collective-permute-start | bytes 786440 | tf_op jit(solution)/shard_map/ppermute | solution.py:23
  89.7 2.7 %collective-permute-done.9 = bf16[256,512]{1,0:T(8,128)(2,1)S(1)} collective-permute-done((bf16[256,512]{1,0:T(8,128)(2,1)}, bf16[256,512]{1,0:T(8,128)(2,1)S(1)}, u32[]{:S(2)}, u32[]{:S(2)}) %collective-permute-start.9) | collective-permute-done | bytes 262176 | tf_op jit(solution)/shard_map/ppermute | solution.py:23
  92.4 2.0 %collective-permute-done.11 = bf16[256,512]{1,0:T(8,128)(2,1)S(1)} collective-permute-done((bf16[256,512]{1,0:T(8,128)(2,1)S(1)}, bf16[256,512]{1,0:T(8,128)(2,1)S(1)}, u32[]{:S(2)}, u32[]{:S(2)}) %collective-permute-start.11) | collective-permute-done | bytes 262176 | tf_op jit(solution)/shard_map/ppermute | solution.py:23
  94.4 3.4 %collective-permute-done.8 = bf16[256,512]{1,0:T(8,128)(2,1)S(1)} collective-permute-done((bf16[256,512]{1,0:T(8,128)(2,1)S(1)}, bf16[256,512]{1,0:T(8,128)(2,1)S(1)}, u32[]{:S(2)}, u32[]{:S(2)}) %collective-permute-start.8) | collective-permute-done | bytes 262176 | tf_op jit(solution)/shard_map/ppermute | solution.py:23
  97.8 2.0 %add_convert_fusion.4 = (bf16[256,512]{1,0:T(8,128)(2,1)}, bf16[256,512]{1,0:T(8,128)(2,1)S(1)}) fusion(bf16[256,512]{1,0:T(8,128)(2,1)S(1)} %collective-permute-done.11, bf16[256,512]{1,0:T(8,128)(2,1)S(1)} %collective-permute-done.9, bf16[256,512]{1,0:T(8,128)(2,1)} %get-tuple-element.32, bf16[512,512]{1,0:T(8,128)(2,1)S(1)} %copy-done.6, ...), kind=kLoop, calls=%fused_computation.6 | loop fusion | flops 2097152 | bytes 2621440 | tf_op jit(solution)/shard_map/convert_element_type | solution.py:525
  99.8 3.2 %collective-permute-start.15 = (bf16[256,512]{1,0:T(8,128)(2,1)}, bf16[256,512]{1,0:T(8,128)(2,1)}, u32[]{:S(2)}, u32[]{:S(2)}) collective-permute-start(bf16[256,512]{1,0:T(8,128)(2,1)} %get-tuple-element.44.o1), channel_id=1, source_target_pairs={{0,3},{1,0},{2,1},{3,2},{4,7},{5,4},{6,5},{7,6},{8,11},{9,8},{10,9... | collective-permute-start | bytes 786440 | tf_op jit(solution)/shard_map/ppermute | solution.py:23
  103.0 3.2 %collective-permute-start.14 = (bf16[256,512]{1,0:T(8,128)(2,1)S(1)}, bf16[256,512]{1,0:T(8,128)(2,1)}, u32[]{:S(2)}, u32[]{:S(2)}) collective-permute-start(bf16[256,512]{1,0:T(8,128)(2,1)S(1)} %get-tuple-element.45.o0), channel_id=1, source_target_pairs={{0,3},{1,0},{2,1},{3,2},{4,7},{5,4},{6,5},{7,6},{8,11},{9,8},{10,9... | collective-permute-start | bytes 786440 | tf_op jit(solution)/shard_map/ppermute | solution.py:23
  106.3 4.0 %collective-permute-done.12.l0 = bf16[256,512]{1,0:T(8,128)(2,1)} collective-permute-done((bf16[256,512]{1,0:T(8,128)(2,1)S(1)}, bf16[256,512]{1,0:T(8,128)(2,1)}, u32[]{:S(2)}, u32[]{:S(2)}) %collective-permute-start.12) | collective-permute-done | bytes 262176 | tf_op jit(solution)/shard_map/ppermute | solution.py:23
  110.3 3.4 %collective-permute-start.17 = (bf16[256,512]{1,0:T(8,128)(2,1)}, bf16[256,512]{1,0:T(8,128)(2,1)}, u32[]{:S(2)}, u32[]{:S(2)}) collective-permute-start(bf16[256,512]{1,0:T(8,128)(2,1)} %collective-permute-done.15.r1), channel_id=1, source_target_pairs={{0,3},{1,0},{2,1},{3,2},{4,7},{5,4},{6,5},{7,6},{8,11},{9,8},{10,9... | collective-permute-start | bytes 786440 | tf_op jit(solution)/shard_map/ppermute | solution.py:23
  114.9 6.3 %copy.20 = bf16[2048,2,768]{2,0,1:T(8,128)(2,1)} copy(bf16[2048,2,768]{2,1,0:T(2,128)(2,1)} %param.22) | data formatting | bytes 12582912 | tf_op args[8]
  121.2 11.1 %feed_forward.1 = (bf16[256,512]{1,0:T(8,128)(2,1)}, bf16[256,512]{1,0:T(8,128)(2,1)}, bf16[256,512]{1,0:T(8,128)(2,1)}, bf16[256,512]{1,0:T(8,128)(2,1)}, bf16[...) custom-call(bf16[256,512]{1,0:T(8,128)(2,1)} %copy-done.3, ...), custom_call_target="tpu_custom_call" | custom-call | tf_op jit(solution)/shard_map/feed_forward/pallas_call | solution.py:258
  136.1 3.3 %reorder.1 = bf16[32,2,16,2,256]{4,3,2,1,0:T(2,128)(2,1)} custom-call(s32[32]{0:T(128)} %slot_map.5, bf16[32,96,2,256]{3,2,1,0:T(2,128)(2,1)} %copy-done), custom_call_target="tpu_custom_call" | custom-call | tf_op jit(solution)/shard_map/reorder/pallas_call | solution.py:387
  139.4 7.4 %all-to-all-start.2 = ((bf16[32,2,16,2,256]{4,3,2,1,0:T(2,128)(2,1)}), bf16[32,2,16,2,256]{4,3,2,1,0:T(2,128)(2,1)S(1)}, u32[]{:S(2)}, u32[]{:S(2)}) async-start(bf16[32,2,16,2,256]{4,3,2,1,0:T(2,128)(2,1)} %reorder.1), calls=%async_computation.2 | async-start | bytes 2097152 | tf_op jit(solution)/shard_map/all_to_all | solution.py:483
  147.9 3.3 %collective-permute-start.23 = (bf16[256,512]{1,0:T(8,128)(2,1)S(1)}, bf16[256,512]{1,0:T(8,128)(2,1)S(1)}, u32[]{:S(2)}, u32[]{:S(2)}) collective-permute-start(bf16[256,512]{1,0:T(8,128)(2,1)S(1)} %add_convert_fusion.1), channel_id=1, source_target_pairs={{0,3},{1,0},{2,1},{3,2},{4,7},{5,4},{6,5},{7,6},{8,11},{9,8},{10,9... | collective-permute-start | bytes 786440 | tf_op jit(solution)/shard_map/ppermute | solution.py:23
  152.7 1.7 %collective-permute-start.20 = (bf16[256,512]{1,0:T(8,128)(2,1)S(1)}, bf16[256,512]{1,0:T(8,128)(2,1)S(1)}, u32[]{:S(2)}, u32[]{:S(2)}) collective-permute-start(bf16[256,512]{1,0:T(8,128)(2,1)S(1)} %add_convert_fusion.3), channel_id=1, source_target_pairs={{0,1},{1,2},{2,3},{3,0},{4,5},{5,6},{6,7},{7,4},{8,9},{9,10},{10,1... | collective-permute-start | bytes 786440 | tf_op jit(solution)/shard_map/ppermute | solution.py:23
  155.2 2.7 %collective-permute-done.23 = bf16[256,512]{1,0:T(8,128)(2,1)S(1)} collective-permute-done((bf16[256,512]{1,0:T(8,128)(2,1)S(1)}, bf16[256,512]{1,0:T(8,128)(2,1)S(1)}, u32[]{:S(2)}, u32[]{:S(2)}) %collective-permute-start.23) | collective-permute-done | bytes 262176 | tf_op jit(solution)/shard_map/ppermute | solution.py:23
  159.1 3.9 %collective-permute-done.18 = bf16[256,512]{1,0:T(8,128)(2,1)S(1)} collective-permute-done((bf16[256,512]{1,0:T(8,128)(2,1)}, bf16[256,512]{1,0:T(8,128)(2,1)S(1)}, u32[]{:S(2)}, u32[]{:S(2)}) %collective-permute-start.18) | collective-permute-done | bytes 262176 | tf_op jit(solution)/shard_map/ppermute | solution.py:23
  165.0 5.1 %pages.1 = bf16[1,12,256,2,256]{4,3,2,1,0:T(2,128)(2,1)} custom-call(s32[32]{0:T(128)} %slot_map.5, s32[32]{0:T(128)} %prior_len.1, s32[192]{0:T(256)} %reshape.56.table, bf16[32,96,2,256]{3,2,1,0:T(2,128)(2,1)} %copy-done, bf16[32,2,16,2,256]{4,3,2,1,0:T(2,128)(2,1)} %copy-done.2), custom_call_target="tpu_custom_call" | custom-call | tf_op jit(solution)/shard_map/pages/pallas_call | solution.py:451
  (90 shorter events, 22.2 us)
Async XLA Ops:
  0.7 38.6 %all-to-all-start = ((bf16[32,32,2,512]{3,2,1,0:T(2,128)(2,1)}), bf16[32,32,2,512]{3,2,1,0:T(2,128)(2,1)S(1)}, u32[]{:S(2)}, u32[]{:S(2)}) async-start(bf16[32,32,2,512]{3,2,1,0:T(2,128)(2,1)} %bitcast.8), calls=%async_computation | async-start | bytes 4194304 | tf_op jit(solution)/shard_map/all_to_all | solution.py:483
  9.2 10.5 %collective-permute-start = (bf16[256,512]{1,0:T(8,128)(2,1)S(1)}, bf16[256,512]{1,0:T(8,128)(2,1)S(1)}, u32[]{:S(2)}, u32[]{:S(2)}) collective-permute-start(bf16[256,512]{1,0:T(8,128)(2,1)S(1)} %get-tuple-element.47.o0), channel_id=1, source_target_pairs={{0,1},{1,2},{2,3},{3,0},{4,5},{5,6},{6,7},{7,4},{8,9},{9,10},{10,1... | collective-permute-start | bytes 786440 | tf_op jit(solution)/shard_map/ppermute | solution.py:23
  10.8 9.2 %collective-permute-start.3 = (bf16[256,512]{1,0:T(8,128)(2,1)S(1)}, bf16[256,512]{1,0:T(8,128)(2,1)S(1)}, u32[]{:S(2)}, u32[]{:S(2)}) collective-permute-start(bf16[256,512]{1,0:T(8,128)(2,1)S(1)} %get-tuple-element.46.o1), channel_id=1, source_target_pairs={{0,3},{1,0},{2,1},{3,2},{4,7},{5,4},{6,5},{7,6},{8,11},{9,8},{10,9... | collective-permute-start | bytes 786440 | tf_op jit(solution)/shard_map/ppermute | solution.py:23
  12.5 13.5 %collective-permute-start.1 = (bf16[256,512]{1,0:T(8,128)(2,1)S(1)}, bf16[256,512]{1,0:T(8,128)(2,1)S(1)}, u32[]{:S(2)}, u32[]{:S(2)}) collective-permute-start(bf16[256,512]{1,0:T(8,128)(2,1)S(1)} %get-tuple-element.46.o1), channel_id=1, source_target_pairs={{0,1},{1,2},{2,3},{3,0},{4,5},{5,6},{6,7},{7,4},{8,9},{9,10},{10,1... | collective-permute-start | bytes 786440 | tf_op jit(solution)/shard_map/ppermute | solution.py:23
  12.8 13.1 %collective-permute-start.2 = (bf16[256,512]{1,0:T(8,128)(2,1)S(1)}, bf16[256,512]{1,0:T(8,128)(2,1)}, u32[]{:S(2)}, u32[]{:S(2)}) collective-permute-start(bf16[256,512]{1,0:T(8,128)(2,1)S(1)} %get-tuple-element.47.o0), channel_id=1, source_target_pairs={{0,3},{1,0},{2,1},{3,2},{4,7},{5,4},{6,5},{7,6},{8,11},{9,8},{10,9... | collective-permute-start | bytes 786440 | tf_op jit(solution)/shard_map/ppermute | solution.py:23
  19.6 10.7 %collective-permute-start.4 = (bf16[256,512]{1,0:T(8,128)(2,1)S(1)}, bf16[256,512]{1,0:T(8,128)(2,1)}, u32[]{:S(2)}, u32[]{:S(2)}) collective-permute-start(bf16[256,512]{1,0:T(8,128)(2,1)S(1)} %collective-permute-done.l0), channel_id=1, source_target_pairs={{0,1},{1,2},{2,3},{3,0},{4,5},{5,6},{6,7},{7,4},{8,9},{9,10},{10,1... | collective-permute-start | bytes 786440 | tf_op jit(solution)/shard_map/ppermute | solution.py:23
  20.0 10.4 %collective-permute-start.5 = (bf16[256,512]{1,0:T(8,128)(2,1)S(1)}, bf16[256,512]{1,0:T(8,128)(2,1)}, u32[]{:S(2)}, u32[]{:S(2)}) collective-permute-start(bf16[256,512]{1,0:T(8,128)(2,1)S(1)} %collective-permute-done.3.r1), channel_id=1, source_target_pairs={{0,3},{1,0},{2,1},{3,2},{4,7},{5,4},{6,5},{7,6},{8,11},{9,8},{10,9... | collective-permute-start | bytes 786440 | tf_op jit(solution)/shard_map/ppermute | solution.py:23
  45.6 88.8 %all-to-all-start.1 = ((bf16[32,96,2,256]{3,2,1,0:T(2,128)(2,1)}), bf16[32,96,2,256]{3,2,1,0:T(2,128)(2,1)S(1)}, u32[]{:S(2)}, u32[]{:S(2)}) async-start(bf16[32,96,2,256]{3,2,1,0:T(2,128)(2,1)} %mix.1), calls=%async_computation.1 | async-start | bytes 6291456 | tf_op jit(solution)/shard_map/all_to_all | solution.py:483
  57.7 40.1 %copy-start.6 = (bf16[512,512]{1,0:T(8,128)(2,1)S(1)}, bf16[512,512]{1,0:T(8,128)(2,1)}, u32[]{:S(2)}) copy-start(bf16[512,512]{1,0:T(8,128)(2,1)} %param.14) | copy-start | bytes 1572868
  73.8 39.9 %copy-start.16 = (f32[2048]{0:T(1024)S(1)}, f32[2048]{0:T(1024)}, u32[]{:S(2)}) copy-start(f32[2048]{0:T(1024)} %param.20) | copy-start | bytes 24580
  73.8 40.5 %copy-start.17 = (f32[2048]{0:T(1024)S(1)}, f32[2048]{0:T(1024)}, u32[]{:S(2)}) copy-start(f32[2048]{0:T(1024)} %param.21) | copy-start | bytes 24580
  73.8 10.1 %collective-permute-start.10 = (bf16[256,512]{1,0:T(8,128)(2,1)}, bf16[256,512]{1,0:T(8,128)(2,1)S(1)}, u32[]{:S(2)}, u32[]{:S(2)}) collective-permute-start(bf16[256,512]{1,0:T(8,128)(2,1)} %get-tuple-element.35), channel_id=1, source_target_pairs={{0,3},{1,0},{2,1},{3,2},{4,7},{5,4},{6,5},{7,6},{8,11},{9,8},{10,9... | collective-permute-start | bytes 786440 | tf_op jit(solution)/shard_map/ppermute | solution.py:23
  76.9 11.7 %collective-permute-start.7 = (bf16[256,512]{1,0:T(8,128)(2,1)}, bf16[256,512]{1,0:T(8,128)(2,1)S(1)}, u32[]{:S(2)}, u32[]{:S(2)}) collective-permute-start(bf16[256,512]{1,0:T(8,128)(2,1)} %get-tuple-element.31), channel_id=1, source_target_pairs={{0,1},{1,2},{2,3},{3,0},{4,5},{5,6},{6,7},{7,4},{8,9},{9,10},{10,1... | collective-permute-start | bytes 786440 | tf_op jit(solution)/shard_map/ppermute | solution.py:23
  76.9 15.5 %collective-permute-start.9 = (bf16[256,512]{1,0:T(8,128)(2,1)}, bf16[256,512]{1,0:T(8,128)(2,1)S(1)}, u32[]{:S(2)}, u32[]{:S(2)}) collective-permute-start(bf16[256,512]{1,0:T(8,128)(2,1)} %get-tuple-element.33), channel_id=1, source_target_pairs={{0,1},{1,2},{2,3},{3,0},{4,5},{5,6},{6,7},{7,4},{8,9},{9,10},{10,1... | collective-permute-start | bytes 786440 | tf_op jit(solution)/shard_map/ppermute | solution.py:23
  77.5 14.9 %collective-permute-start.6 = (bf16[256,512]{1,0:T(8,128)(2,1)}, bf16[256,512]{1,0:T(8,128)(2,1)S(1)}, u32[]{:S(2)}, u32[]{:S(2)}) collective-permute-start(bf16[256,512]{1,0:T(8,128)(2,1)} %get-tuple-element.29), channel_id=1, source_target_pairs={{0,3},{1,0},{2,1},{3,2},{4,7},{5,4},{6,5},{7,6},{8,11},{9,8},{10,9... | collective-permute-start | bytes 786440 | tf_op jit(solution)/shard_map/ppermute | solution.py:23
  84.9 9.4 %collective-permute-start.11 = (bf16[256,512]{1,0:T(8,128)(2,1)S(1)}, bf16[256,512]{1,0:T(8,128)(2,1)S(1)}, u32[]{:S(2)}, u32[]{:S(2)}) collective-permute-start(bf16[256,512]{1,0:T(8,128)(2,1)S(1)} %add_convert_fusion.5), channel_id=1, source_target_pairs={{0,3},{1,0},{2,1},{3,2},{4,7},{5,4},{6,5},{7,6},{8,11},{9,8},{10,9... | collective-permute-start | bytes 786440 | tf_op jit(solution)/shard_map/ppermute | solution.py:23
  89.6 8.2 %collective-permute-start.8 = (bf16[256,512]{1,0:T(8,128)(2,1)S(1)}, bf16[256,512]{1,0:T(8,128)(2,1)S(1)}, u32[]{:S(2)}, u32[]{:S(2)}) collective-permute-start(bf16[256,512]{1,0:T(8,128)(2,1)S(1)} %add_convert_fusion.7), channel_id=1, source_target_pairs={{0,1},{1,2},{2,3},{3,0},{4,5},{5,6},{6,7},{7,4},{8,9},{9,10},{10,1... | collective-permute-start | bytes 786440 | tf_op jit(solution)/shard_map/ppermute | solution.py:23
  99.8 10.5 %collective-permute-start.12 = (bf16[256,512]{1,0:T(8,128)(2,1)S(1)}, bf16[256,512]{1,0:T(8,128)(2,1)}, u32[]{:S(2)}, u32[]{:S(2)}) collective-permute-start(bf16[256,512]{1,0:T(8,128)(2,1)S(1)} %get-tuple-element.45.o0), channel_id=1, source_target_pairs={{0,1},{1,2},{2,3},{3,0},{4,5},{5,6},{6,7},{7,4},{8,9},{9,10},{10,1... | collective-permute-start | bytes 786440 | tf_op jit(solution)/shard_map/ppermute | solution.py:23
  99.8 10.5 %collective-permute-start.15 = (bf16[256,512]{1,0:T(8,128)(2,1)}, bf16[256,512]{1,0:T(8,128)(2,1)}, u32[]{:S(2)}, u32[]{:S(2)}) collective-permute-start(bf16[256,512]{1,0:T(8,128)(2,1)} %get-tuple-element.44.o1), channel_id=1, source_target_pairs={{0,3},{1,0},{2,1},{3,2},{4,7},{5,4},{6,5},{7,6},{8,11},{9,8},{10,9... | collective-permute-start | bytes 786440 | tf_op jit(solution)/shard_map/ppermute | solution.py:23
  103.0 18.2 %collective-permute-start.13 = (bf16[256,512]{1,0:T(8,128)(2,1)}, bf16[256,512]{1,0:T(8,128)(2,1)}, u32[]{:S(2)}, u32[]{:S(2)}) collective-permute-start(bf16[256,512]{1,0:T(8,128)(2,1)} %get-tuple-element.44.o1), channel_id=1, source_target_pairs={{0,1},{1,2},{2,3},{3,0},{4,5},{5,6},{6,7},{7,4},{8,9},{9,10},{10,1... | collective-permute-start | bytes 786440 | tf_op jit(solution)/shard_map/ppermute | solution.py:23
  103.0 18.2 %collective-permute-start.14 = (bf16[256,512]{1,0:T(8,128)(2,1)S(1)}, bf16[256,512]{1,0:T(8,128)(2,1)}, u32[]{:S(2)}, u32[]{:S(2)}) collective-permute-start(bf16[256,512]{1,0:T(8,128)(2,1)S(1)} %get-tuple-element.45.o0), channel_id=1, source_target_pairs={{0,3},{1,0},{2,1},{3,2},{4,7},{5,4},{6,5},{7,6},{8,11},{9,8},{10,9... | collective-permute-start | bytes 786440 | tf_op jit(solution)/shard_map/ppermute | solution.py:23
  110.3 10.9 %collective-permute-start.16 = (bf16[256,512]{1,0:T(8,128)(2,1)}, bf16[256,512]{1,0:T(8,128)(2,1)}, u32[]{:S(2)}, u32[]{:S(2)}) collective-permute-start(bf16[256,512]{1,0:T(8,128)(2,1)} %collective-permute-done.12.l0), channel_id=1, source_target_pairs={{0,1},{1,2},{2,3},{3,0},{4,5},{5,6},{6,7},{7,4},{8,9},{9,10},{10,1... | collective-permute-start | bytes 786440 | tf_op jit(solution)/shard_map/ppermute | solution.py:23
  110.3 10.9 %collective-permute-start.17 = (bf16[256,512]{1,0:T(8,128)(2,1)}, bf16[256,512]{1,0:T(8,128)(2,1)}, u32[]{:S(2)}, u32[]{:S(2)}) collective-permute-start(bf16[256,512]{1,0:T(8,128)(2,1)} %collective-permute-done.15.r1), channel_id=1, source_target_pairs={{0,3},{1,0},{2,1},{3,2},{4,7},{5,4},{6,5},{7,6},{8,11},{9,8},{10,9... | collective-permute-start | bytes 786440 | tf_op jit(solution)/shard_map/ppermute | solution.py:23
  132.3 14.5 %collective-permute-start.22 = (bf16[256,512]{1,0:T(8,128)(2,1)}, bf16[256,512]{1,0:T(8,128)(2,1)}, u32[]{:S(2)}, u32[]{:S(2)}) collective-permute-start(bf16[256,512]{1,0:T(8,128)(2,1)} %get-tuple-element.43), channel_id=1, source_target_pairs={{0,3},{1,0},{2,1},{3,2},{4,7},{5,4},{6,5},{7,6},{8,11},{9,8},{10,9... | collective-permute-start | bytes 786440 | tf_op jit(solution)/shard_map/ppermute | solution.py:23
  132.8 18.8 %collective-permute-start.19 = (bf16[256,512]{1,0:T(8,128)(2,1)}, bf16[256,512]{1,0:T(8,128)(2,1)}, u32[]{:S(2)}, u32[]{:S(2)}) collective-permute-start(bf16[256,512]{1,0:T(8,128)(2,1)} %get-tuple-element.39), channel_id=1, source_target_pairs={{0,1},{1,2},{2,3},{3,0},{4,5},{5,6},{6,7},{7,4},{8,9},{9,10},{10,1... | collective-permute-start | bytes 786440 | tf_op jit(solution)/shard_map/ppermute | solution.py:23
  134.4 20.8 %collective-permute-start.21 = (bf16[256,512]{1,0:T(8,128)(2,1)}, bf16[256,512]{1,0:T(8,128)(2,1)}, u32[]{:S(2)}, u32[]{:S(2)}) collective-permute-start(bf16[256,512]{1,0:T(8,128)(2,1)} %get-tuple-element.41), channel_id=1, source_target_pairs={{0,1},{1,2},{2,3},{3,0},{4,5},{5,6},{6,7},{7,4},{8,9},{9,10},{10,1... | collective-permute-start | bytes 786440 | tf_op jit(solution)/shard_map/ppermute | solution.py:23
  139.4 23.5 %copy-start.4 = (bf16[256,512]{1,0:T(8,128)(2,1)S(1)}, bf16[256,512]{1,0:T(8,128)(2,1)}, u32[]{:S(2)}) copy-start(bf16[256,512]{1,0:T(8,128)(2,1)} %copy-done.3) | copy-start | bytes 786436
  139.4 23.5 %copy-start.9 = (bf16[256,512]{1,0:T(8,128)(2,1)S(1)}, bf16[256,512]{1,0:T(8,128)(2,1)}, u32[]{:S(2)}) copy-start(bf16[256,512]{1,0:T(8,128)(2,1)} %get-tuple-element.36) | copy-start | bytes 786436
  139.4 24.6 %all-to-all-start.2 = ((bf16[32,2,16,2,256]{4,3,2,1,0:T(2,128)(2,1)}), bf16[32,2,16,2,256]{4,3,2,1,0:T(2,128)(2,1)S(1)}, u32[]{:S(2)}, u32[]{:S(2)}) async-start(bf16[32,2,16,2,256]{4,3,2,1,0:T(2,128)(2,1)} %reorder.1), calls=%async_computation.2 | async-start | bytes 2097152 | tf_op jit(solution)/shard_map/all_to_all | solution.py:483
  147.9 10.0 %collective-permute-start.23 = (bf16[256,512]{1,0:T(8,128)(2,1)S(1)}, bf16[256,512]{1,0:T(8,128)(2,1)S(1)}, u32[]{:S(2)}, u32[]{:S(2)}) collective-permute-start(bf16[256,512]{1,0:T(8,128)(2,1)S(1)} %add_convert_fusion.1), channel_id=1, source_target_pairs={{0,3},{1,0},{2,1},{3,2},{4,7},{5,4},{6,5},{7,6},{8,11},{9,8},{10,9... | collective-permute-start | bytes 786440 | tf_op jit(solution)/shard_map/ppermute | solution.py:23
  151.2 11.7 %collective-permute-start.18 = (bf16[256,512]{1,0:T(8,128)(2,1)}, bf16[256,512]{1,0:T(8,128)(2,1)S(1)}, u32[]{:S(2)}, u32[]{:S(2)}) collective-permute-start(bf16[256,512]{1,0:T(8,128)(2,1)} %get-tuple-element.37), channel_id=1, source_target_pairs={{0,3},{1,0},{2,1},{3,2},{4,7},{5,4},{6,5},{7,6},{8,11},{9,8},{10,9... | collective-permute-start | bytes 786440 | tf_op jit(solution)/shard_map/ppermute | solution.py:23
  152.7 10.3 %collective-permute-start.20 = (bf16[256,512]{1,0:T(8,128)(2,1)S(1)}, bf16[256,512]{1,0:T(8,128)(2,1)S(1)}, u32[]{:S(2)}, u32[]{:S(2)}) collective-permute-start(bf16[256,512]{1,0:T(8,128)(2,1)S(1)} %add_convert_fusion.3), channel_id=1, source_target_pairs={{0,1},{1,2},{2,3},{3,0},{4,5},{5,6},{6,7},{7,4},{8,9},{9,10},{10,1... | collective-permute-start | bytes 786440 | tf_op jit(solution)/shard_map/ppermute | solution.py:23
  (15 other events, 205.4 us)
where the time goes:
time: 172 us; the launch traced here: 170 us
  starting transfers between devices  60.3 us (35%)
  Pallas kernels  54.2 us (32%)
  waiting for transfers between devices  29.6 us (17%)
  local copies, waits for them, and re-layouts  14.1 us (8%)
  other arithmetic  10.9 us (6%)
    ppermute x24, starting transfers between devices, shift_by(): return lax.ppermute(value, 'tp', [(i, (i + step) % 4) for i in range(4)])  37.2 us
    ppermute x24, waiting for transfers between devices, shift_by(): return lax.ppermute(value, 'tp', [(i, (i + step) % 4) for i in range(4)])  29.5 us
    all_to_all x3, starting transfers between devices, exchange(): lax.all_to_all(pieces, 'req', split_axis=0, concat_axis=0, tiled=True)  23 us
    pallas_call x1, Pallas kernels, attend(): pl.pallas_call(attend_kernel, out_shape=(jax.ShapeDtypeStruct((rows // 2,...  16.1 us
    pallas_call x1, Pallas kernels, feed_forward(): pl.pallas_call(forward_kernel, out_shape=(jax.ShapeDtypeStruct((half, wid...  11.1 us
    unnamed x42, local copies, waits for them, and re-layouts  10.4 us
    pallas_call x1, Pallas kernels, project(): pl.pallas_call(project_kernel, out_shape=(out, out, out), in_specs=specs(...  8.84 us
    pallas_call x1, Pallas kernels, pages(): pl.pallas_call(pages_kernel, out_shape=jax.ShapeDtypeStruct((1, 2 * (cach...  5.06 us
  transfers between devices with their start and end apart: 27, of which 10 were waited for; matrix products, arithmetic and copies ran while one was open for 12% of the time, Pallas kernels for 26%

commit v1 on v0

--- a/solution.py
+++ b/solution.py
@@ -23,28 +23,52 @@
     return lax.ppermute(value, "tp", [(i, (i + step) % 4) for i in range(4)])
 
 
-def ring_gather(top, bottom):
-    left_top = shift_by(top, 1)
-    right_bottom = shift_by(bottom, -1)
-    left_bottom = shift_by(bottom, 1)
-    right_top = shift_by(top, -1)
-    far_top = shift_by(left_top, 1)
-    far_bottom = shift_by(right_bottom, -1)
-    return (top, bottom, left_top, left_bottom, right_top, right_bottom, far_top, far_bottom)
-
-
-def ring_scatter(parts):
-    own_top, own_bottom, left_top, left_bottom, right_top, right_bottom, far_top, far_bottom = parts
-    add = lambda a, b: (a.astype(F32) + b.astype(F32))
-    far_top = shift_by(far_top, 1)
-    far_bottom = shift_by(far_bottom, -1)
-    from_left_bottom = shift_by(right_bottom, 1)
-    from_right_top = shift_by(left_top, -1)
-    from_left_top = shift_by(add(right_top, far_top).astype(BF), 1)
-    from_right_bottom = shift_by(add(left_bottom, far_bottom).astype(BF), -1)
-    top = add(own_top, from_right_top) + from_left_top.astype(F32)
-    bottom = add(own_bottom, from_left_bottom) + from_right_bottom.astype(F32)
-    return top, bottom
+def ring_gather(own):
+    half = own.shape[0] // 2
+    left = shift_by(own, 1)
+    right = shift_by(own, -1)
+    far_top = shift_by(left[:half], 1)
+    far_bottom = shift_by(right[half:], -1)
+    return own, left, right, far_top, far_bottom
+
+
+def add(*terms):
+    total = terms[0].astype(F32)
+    for term in terms[1:]:
+        total = total + term.astype(F32)
+    return total
+
+
+def ring_scatter(base, own, to_right, to_left, right_top, left_bottom):
+    half = own.shape[0] // 2
+    from_left = shift_by(to_right, 1)
+    from_right = shift_by(to_left, -1)
+    last_top = shift_by(add(right_top, from_left[:half]).astype(BF), 1)
+    last_bottom = shift_by(add(left_bottom, from_right[half:]).astype(BF), -1)
+    top = add(own[:half], from_right[:half], last_top)
+    bottom = add(own[half:], from_left[half:], last_bottom)
+    return (base.astype(F32) + jnp.concatenate([top, bottom], axis=0)).astype(BF)
+
+
+def store_product(outs, slot, part, half, value):
+    own, to_right, to_left, right_top, left_bottom = outs
+    place = {
+        (0, 0): (own, 0),
+        (0, 1): (own, half),
+        (1, 0): (to_left, 0),
+        (1, 1): (left_bottom, 0),
+        (2, 0): (right_top, 0),
+        (2, 1): (to_right, half),
+        (3, 0): (to_right, 0),
+        (3, 1): (to_left, half),
+    }
+    ref, at = place[slot, part]
+    ref[at : at + half, :] = value.astype(BF)
+
+
+def product_shapes(rows, width):
+    whole, half = jax.ShapeDtypeStruct((rows, width), BF), jax.ShapeDtypeStruct((rows // 2, width), BF)
+    return (whole, whole, whole, half, half)
 
 
 def norm_into(normed, pieces, gain, shift, blocks, half):
@@ -52,7 +76,9 @@
     total = 4 * width
     step = 64
     for part in range(2):
-        refs = pieces[part::2]
+        own, left, right, far_top, far_bottom = pieces
+        refs = [ref.at[part * half : (part + 1) * half] for ref in (own, left, right)]
+        refs.append((far_top, far_bottom)[part])
 
         def body(index, carry, refs=refs, part=part):
             at = pl.multiple_of(index * step, step)
@@ -71,11 +97,10 @@
 
 
 def project_kernel(
-    o0, o1, l0, l1, r0, r1, f0, f1, gain, shift, weight, bias, cosine, sine_a, sine_b, queries, keys, values, buffer, normed, sems
+    own, left, right, far_top, far_bottom, gain, shift, weight, bias, cosine, sine_a, sine_b, queries, keys, values, buffer, normed, sems
 ):
     device = lax.axis_index("tp")
-    width = o0.shape[1]
-    half = o0.shape[0]
+    half, width = far_top.shape
     blocks = [lax.rem(device + offset, 4) for offset in OFFSETS]
     copies = []
     for slot in range(4):
@@ -87,7 +112,7 @@
             )
         )
         copies[-1].start()
-    norm_into(normed, (o0, o1, l0, l1, r0, r1, f0, f1), gain, shift, blocks, half)
+    norm_into(normed, (own, left, right, far_top, far_bottom), gain, shift, blocks, half)
     for copy in copies:
         copy.wait()
     outs = (queries, keys, values)
@@ -115,7 +140,7 @@
 
 
 def specs(*kinds):
-    table = {"v": pl.BlockSpec(memory_space=VMEM), "s": pl.BlockSpec(memory_space=SMEM), "a": pl.BlockSpec(memory_space=pl.ANY)}
+    table = {"v": pl.BlockSpec(memory_space=VMEM), "s": pl.BlockSpec(memory_space=SMEM), "a": pl.BlockSpec(memory_space=pltpu.MemorySpace.HBM)}
     return [table[kind] for kind in kinds]
 
 
@@ -123,12 +148,12 @@
 
 
 def project(pieces, gain, shift, weight, bias, tables):
-    half, width = pieces[0].shape
+    half, width = pieces[-1].shape
     out = jax.ShapeDtypeStruct((2 * half, width), BF)
     return pl.pallas_call(
         project_kernel,
         out_shape=(out, out, out),
-        in_specs=specs(*"v" * 8, "v", "v", "a", "v", "v", "v", "v"),
+        in_specs=specs(*"v" * 5, "v", "v", "a", "v", "v", "v", "v"),
         out_specs=tuple(specs("v", "v", "v")),
         scratch_shapes=[
             pltpu.VMEM((3, 4 * width, width), BF),
@@ -141,7 +166,7 @@
 
 
 def attend_kernel(lengths, queries, new_keys, new_values, old_keys, old_values, weight, *refs):
-    outs, (buffer, mixed, sems) = refs[:8], refs[8:]
+    outs, (buffer, mixed, sems) = refs[:5], refs[5:]
     device = lax.axis_index("tp")
     prior = lengths[lax.axis_index("req")]
     rows_all, width = queries.shape
@@ -199,26 +224,26 @@
         rows = slice(part * step, (part + 1) * step)
         for slot in range(4):
             product = jnp.dot(mixed[rows, :], buffer[:, slot * width : (slot + 1) * width], preferred_element_type=F32)
-            outs[2 * slot + part][...] = product.astype(BF)
+            store_product(outs, slot, part, step, product)
 
 
 def attend(lengths, queries, new_keys, new_values, old_keys, old_values, weight):
     rows, width = queries.shape
     return pl.pallas_call(
         attend_kernel,
-        out_shape=(jax.ShapeDtypeStruct((rows // 2, width), BF),) * 8,
+        out_shape=product_shapes(rows, width),
         in_specs=specs("s", "v", "v", "v", "v", "v", "a"),
-        out_specs=tuple(specs(*"v" * 8)),
+        out_specs=tuple(specs(*"v" * 5)),
         scratch_shapes=[pltpu.VMEM((width, 4 * width), BF), pltpu.VMEM((rows, width), BF), pltpu.SemaphoreType.DMA((4,))],
         compiler_params=PARAMS,
         name="attend",
     )(lengths, queries, new_keys, new_values, old_keys, old_values, weight)
 
 
-def forward_kernel(o0, o1, l0, l1, r0, r1, f0, f1, gain, shift, expand, contract, *refs):
-    outs, (expand_buffer, contract_buffer, normed, sems) = refs[:8], refs[8:]
+def forward_kernel(own, left, right, far_top, far_bottom, gain, shift, expand, contract, *refs):
+    outs, (expand_buffer, contract_buffer, normed, sems) = refs[:5], refs[5:]
     device = lax.axis_index("tp")
-    half, width = o0.shape
+    half, width = far_top.shape
     blocks = [lax.rem(device + offset, 4) for offset in OFFSETS]
     copies = []
     for slot in range(4):
@@ -239,7 +264,7 @@
         )
     for copy in copies:
         copy.start()
-    norm_into(normed, (o0, o1, l0, l1, r0, r1, f0, f1), gain, shift, blocks, half)
+    norm_into(normed, (own, left, right, far_top, far_bottom), gain, shift, blocks, half)
     for copy in copies:
         copy.wait()
     for part in range(2):
@@ -249,17 +274,17 @@
         hidden = (gate / (1.0 + jnp.exp(-gate)) * up).astype(BF)
         for slot in range(4):
             product = jnp.dot(hidden, contract_buffer[:, slot * width : (slot + 1) * width], preferred_element_type=F32)
-            outs[2 * slot + part][...] = product.astype(BF)
+            store_product(outs, slot, part, half, product)
 
 
 def feed_forward(pieces, gain, shift, expand, contract):
-    half, width = pieces[0].shape
+    half, width = pieces[-1].shape
     hidden = expand.shape[2]
     return pl.pallas_call(
         forward_kernel,
-        out_shape=(jax.ShapeDtypeStruct((half, width), BF),) * 8,
-        in_specs=specs(*"v" * 8, "v", "v", "a", "a"),
-        out_specs=tuple(specs(*"v" * 8)),
+        out_shape=product_shapes(2 * half, width),
+        in_specs=specs(*"v" * 5, "v", "v", "a", "a"),
+        out_specs=tuple(specs(*"v" * 5)),
         scratch_shapes=[
             pltpu.VMEM((2, 4 * width, hidden), BF),
             pltpu.VMEM((hidden, 4 * width), BF),
@@ -501,11 +526,9 @@
 ):
     count = slot_map.shape[0]
     rows, width = tokens.shape
-    half = rows // 2
     cached = prior_cache.shape[1]
     prior_count = prior_len[lax.axis_index("req")]
-    top, bottom = tokens[:half], tokens[half:]
-    pieces = ring_gather(top, bottom)
+    pieces = ring_gather(tokens)
     old = exchange(prior_cache.reshape(count, cached // count, 2, width))
     old_keys, old_values = split(prior_cache[0])
     tables = rotary_tables(prior_count, rows)
@@ -517,26 +540,17 @@
         project_bias,
         tables,
     )
-    parts = attend(prior_len, queries, new_keys, new_values, old_keys, old_values, output_weight)
     mixed = mix(slot_map, old, new_keys, new_values)
     mixed = exchange(mixed)
-    top_sum, bottom_sum = ring_scatter(parts)
-    top = (top.astype(F32) + top_sum).astype(BF)
-    bottom = (bottom.astype(F32) + bottom_sum).astype(BF)
-    pieces = ring_gather(top, bottom)
-    parts = feed_forward(
-        pieces,
-        second_gain.reshape(4, width),
-        second_shift.reshape(4, width),
-        jnp.transpose(expand_weight, (1, 0, 2)),
-        contract_weight,
-    )
+    parts = attend(prior_len, queries, new_keys, new_values, old_keys, old_values, output_weight)
+    residual = ring_scatter(tokens, *parts)
+    expand = jnp.transpose(expand_weight, (1, 0, 2))
+    residual, expand = lax.optimization_barrier((residual, expand))
+    pieces = ring_gather(residual)
+    parts = feed_forward(pieces, second_gain.reshape(4, width), second_shift.reshape(4, width), expand, contract_weight)
     new = reorder(slot_map, mixed, rows // count)
     new = exchange(new)
-    top_sum, bottom_sum = ring_scatter(parts)
-    result = jnp.concatenate(
-        [(top.astype(F32) + top_sum).astype(BF), (bottom.astype(F32) + bottom_sum).astype(BF)], axis=0
-    )
+    result = ring_scatter(residual, *parts)
     page_pool = pages(slot_map, prior_len, block_table.reshape(-1), mixed, new)
     return (result, page_pool)
 

time: 172 us -> 182 us (1.058)
  waiting for transfers between devices: 29.6 us -> 45 us
  starting transfers between devices: 60.3 us -> 49.5 us
  local copies, waits for them, and re-layouts: 14.1 us -> 18.6 us
    ppermute x24 -> x16, waiting for transfers between devices: 29.5 us -> 40.4 us  [shift_by(): return lax.ppermute(value, 'tp', [(i, (i + step) % 4) for i in range(4)])]
    ppermute x24 -> x16, starting transfers between devices: 37.2 us -> 26.6 us  [shift_by(): return lax.ppermute(value, 'tp', [(i, (i + step) % 4) for i in range(4)])]
    all_to_all x3, waiting for transfers between devices: 0.11 us -> 4.62 us  [exchange(): lax.all_to_all(pieces, 'req', split_axis=0, concat_axis=0, tiled=True)]
    add x0 -> x2, other arithmetic: none -> 2.51 us  [add(): total = total + term.astype(F32)]
    slice x1 -> x4, local copies, waits for them, and re-layouts: 0.04 us -> 2.53 us  [the longest x2 1.74 us: ring_gather(): far_bottom = shift_by(right[half:], -1)]
    unnamed x42 -> x48, local copies, waits for them, and re-layouts: 10.4 us -> 12.4 us
    convert_element_type x7 -> x6, other arithmetic: 7.52 us -> 6.15 us  [the longest x2 3 us: ring_scatter(): last_top = shift_by(add(right_top, from_left[:half]).astype(BF), 1)]
  transfers between devices with their start and end apart: 27 -> 19, of which waited for: 10 -> 7; matrix products, arithmetic and copies ran while one was open for 12% -> 13% of each run, Pallas kernels for 26% -> 27%
where the time goes in v1:
time: 182 us; the launch traced here: 180 us
  Pallas kernels  54.2 us (30%)
  starting transfers between devices  49.5 us (27%)
  waiting for transfers between devices  45 us (25%)
  local copies, waits for them, and re-layouts  18.6 us (10%)
  other arithmetic  11.2 us (6%)
    ppermute x16, waiting for transfers between devices, shift_by(): return lax.ppermute(value, 'tp', [(i, (i + step) % 4) for i in range(4)])  40.4 us
    ppermute x16, starting transfers between devices, shift_by(): return lax.ppermute(value, 'tp', [(i, (i + step) % 4) for i in range(4)])  26.6 us
    all_to_all x3, starting transfers between devices, exchange(): lax.all_to_all(pieces, 'req', split_axis=0, concat_axis=0, tiled=True)  22.9 us
    pallas_call x1, Pallas kernels, attend(): pl.pallas_call(attend_kernel, out_shape=product_shapes(rows, width), in_s...  16.1 us
    unnamed x48, local copies, waits for them, and re-layouts  12.4 us
    pallas_call x1, Pallas kernels, feed_forward(): pl.pallas_call(forward_kernel, out_shape=product_shapes(2 * half, width),...  11.1 us
    pallas_call x1, Pallas kernels, project(): pl.pallas_call(project_kernel, out_shape=(out, out, out), in_specs=specs(...  8.84 us
    pallas_call x1, Pallas kernels, pages(): pl.pallas_call(pages_kernel, out_shape=jax.ShapeDtypeStruct((1, 2 * (cach...  5.06 us
  transfers between devices with their start and end apart: 19, of which 7 were waited for; matrix products, arithmetic and copies ran while one was open for 13% of the time, Pallas kernels for 27%

profile of v1, /device:TPU:0, one launch (start us, length us, event | category | flops | bytes accessed | tf_op | source)
XLA Modules:
  0.0 179.7 jit_solution(3491840241059141693)
XLA Ops:
  0.7 8.4 %all-to-all-start = ((bf16[32,32,2,512]{3,2,1,0:T(2,128)(2,1)}), bf16[32,32,2,512]{3,2,1,0:T(2,128)(2,1)S(1)}, u32[]{:S(2)}, u32[]{:S(2)}) async-start(bf16[32,32,2,512]{3,2,1,0:T(2,128)(2,1)} %bitcast.8), calls=%async_computation | async-start | bytes 4194304 | tf_op jit(solution)/shard_map/all_to_all | solution.py:508
  9.1 1.6 collective-permute-start
  10.8 1.7 collective-permute-start.1
  13.7 10.9 %collective-permute-done.left = bf16[512,512]{1,0:T(8,128)(2,1)S(1)} collective-permute-done((bf16[512,512]{1,0:T(8,128)(2,1)S(1)}, bf16[512,512]{1,0:T(8,128)(2,1)S(1)}, u32[]{:S(2)}, u32[]{:S(2)}) %collective-permute-start) | collective-permute-done | bytes 524320 | tf_op jit(solution)/shard_map/ppermute | solution.py:23
  25.9 3.0 %collective-permute-start.3 = (bf16[256,512]{1,0:T(8,128)(2,1)S(1)}, bf16[256,512]{1,0:T(8,128)(2,1)S(1)}, u32[]{:S(2)}, u32[]{:S(2)}) collective-permute-start(bf16[256,512]{1,0:T(8,128)(2,1)S(1)} %slice.65), channel_id=1, source_target_pairs={{0,3},{1,0},{2,1},{3,2},{4,7},{5,4},{6,5},{7,6},{8,11},{9,8},{10,9... | collective-permute-start | bytes 786440 | tf_op jit(solution)/shard_map/ppermute | solution.py:23
  30.2 4.8 %split.1 = (bf16[1024,512]{1,0:T(8,128)(2,1)}, bf16[1024,512]{1,0:T(8,128)(2,1)}) custom-call(bf16[1024,2,512]{2,1,0:T(2,128)(2,1)} %bitcast.9), custom_call_target="tpu_custom_call" | custom-call | tf_op jit(solution)/shard_map/split/pallas_call | solution.py:321
  35.0 1.9 %fusion.2 = (f32[512,128]{1,0:T(8,128)}, f32[512,128]{1,0:T(8,128)}, f32[512,128]{1,0:T(8,128)}) fusion(f32[128]{0:T(128)S(1)} %compare_select_fusion.2, f32[512]{0:T(512)S(1)} %add_convert_fusion.4, pred[128]{0:T(512)(128)(4,1)S(1)} %get-tuple-element.43, pred[128]{0:T(512)(128)(4,1)S(1)} %get-tuple-element.44), kind=kLoop, calls=%fused_computation.15 | loop fusion | flops 262144 | bytes 789248 | tf_op jit(solution)/shard_map/jit(_where)/select_n | solution.py:503
  37.5 8.8 %project.1 = (bf16[512,512]{1,0:T(8,128)(2,1)}, bf16[512,512]{1,0:T(8,128)(2,1)}, bf16[512,512]{1,0:T(8,128)(2,1)}) custom-call(bf16[512,512]{1,0:T(8,128)(2,1)} %own.1, bf16[512,512]{1,0:T(8,128)(2,1)} %copy-done.9, bf16[512,512]{1,0:T(8,128)(2,1)} %collective-permute-done.1.right, bf16[256,512]{1,0:T(8,128)(2,1)} %collective-permute-done.2.far_top, ...), custom_call_target="tpu_custom_call" | custom-call | tf_op jit(solution)/shard_map/project/pallas_call | solution.py:153
  46.4 16.1 %attend.1 = (bf16[512,512]{1,0:T(8,128)(2,1)}, bf16[512,512]{1,0:T(8,128)(2,1)}, bf16[512,512]{1,0:T(8,128)(2,1)}, bf16[256,512]{1,0:T(8,128)(2,1)}, bf16[256,512]{1,0:T(8,128)(2,1)}) custom-call(s32[32]{0:T(128)} %prior_len.1, bf16[512,512]{1,0:T(8,128)(2,1)} %get-tuple-element.19.queries, bf16[512,512]{1,0:T(8,128)(2,1)} %get-tuple-element.20.new_keys.keys, ...), custom_call_target="tpu_custom_call" | custom-call | tf_op jit(solution)/shard_map/attend/pallas_call | solution.py:232
  62.6 3.2 %collective-permute-start.4 = (bf16[512,512]{1,0:T(8,128)(2,1)}, bf16[512,512]{1,0:T(8,128)(2,1)}, u32[]{:S(2)}, u32[]{:S(2)}) collective-permute-start(bf16[512,512]{1,0:T(8,128)(2,1)} %get-tuple-element.25), channel_id=1, source_target_pairs={{0,3},{1,0},{2,1},{3,2},{4,7},{5,4},{6,5},{7,6},{8,11},{9,8},{10,9... | collective-permute-start | bytes 1572872 | tf_op jit(solution)/shard_map/ppermute | solution.py:23
  65.8 1.3 copy-done.1
  67.1 5.0 %mix.1 = bf16[32,96,2,256]{3,2,1,0:T(2,128)(2,1)} custom-call(s32[32]{0:T(128)} %slot_map.5, bf16[32,32,2,512]{3,2,1,0:T(2,128)(2,1)} %copy-done.1, bf16[512,512]{1,0:T(8,128)(2,1)} %get-tuple-element.20.new_keys.keys, bf16[512,512]{1,0:T(8,128)(2,1)} %get-tuple-element.21.new_values.values), custom_call_target="tpu_custom_call" | custom-call | tf_op jit(solution)/shard_map/mix/pallas_call | solution.py:376
  72.1 7.4 %all-to-all-start.1 = ((bf16[32,96,2,256]{3,2,1,0:T(2,128)(2,1)}), bf16[32,96,2,256]{3,2,1,0:T(2,128)(2,1)S(1)}, u32[]{:S(2)}, u32[]{:S(2)}) async-start(bf16[32,96,2,256]{3,2,1,0:T(2,128)(2,1)} %mix.1), calls=%async_computation.1 | async-start | bytes 6291456 | tf_op jit(solution)/shard_map/all_to_all | solution.py:508
  81.8 3.5 %collective-permute-start.7 = (bf16[256,512]{1,0:T(8,128)(2,1)S(1)}, bf16[256,512]{1,0:T(8,128)(2,1)S(1)}, u32[]{:S(2)}, u32[]{:S(2)}) collective-permute-start(bf16[256,512]{1,0:T(8,128)(2,1)S(1)} %add_convert_fusion.2), channel_id=1, source_target_pairs={{0,3},{1,0},{2,1},{3,2},{4,7},{5,4},{6,5},{7,6},{8,11},{9,8},{10,9... | collective-permute-start | bytes 786440 | tf_op jit(solution)/shard_map/ppermute | solution.py:23
  85.3 6.3 %copy.20 = bf16[2048,2,768]{2,0,1:T(8,128)(2,1)} copy(bf16[2048,2,768]{2,1,0:T(2,128)(2,1)} %param.22) | data formatting | bytes 12582912 | tf_op args[8]
  91.5 1.2 convert_add_fusion.3
  93.7 3.1 %collective-permute-start.9 = (bf16[512,512]{1,0:T(8,128)(2,1)S(1)}, bf16[512,512]{1,0:T(8,128)(2,1)S(1)}, u32[]{:S(2)}, u32[]{:S(2)}) collective-permute-start(bf16[512,512]{1,0:T(8,128)(2,1)S(1)} %fusion.own), channel_id=1, source_target_pairs={{0,3},{1,0},{2,1},{3,2},{4,7},{5,4},{6,5},{7,6},{8,11},{9,8},{10,9... | collective-permute-start | bytes 1572872 | tf_op jit(solution)/shard_map/ppermute | solution.py:23
  96.9 10.9 %collective-permute-done.8.left = bf16[512,512]{1,0:T(8,128)(2,1)S(1)} collective-permute-done((bf16[512,512]{1,0:T(8,128)(2,1)S(1)}, bf16[512,512]{1,0:T(8,128)(2,1)S(1)}, u32[]{:S(2)}, u32[]{:S(2)}) %collective-permute-start.8) | collective-permute-done | bytes 524320 | tf_op jit(solution)/shard_map/ppermute | solution.py:23
  109.6 3.1 %collective-permute-start.11 = (bf16[256,512]{1,0:T(8,128)(2,1)}, bf16[256,512]{1,0:T(8,128)(2,1)}, u32[]{:S(2)}, u32[]{:S(2)}) collective-permute-start(bf16[256,512]{1,0:T(8,128)(2,1)} %slice.71), channel_id=1, source_target_pairs={{0,3},{1,0},{2,1},{3,2},{4,7},{5,4},{6,5},{7,6},{8,11},{9,8},{10,9... | collective-permute-start | bytes 786440 | tf_op jit(solution)/shard_map/ppermute | solution.py:23
  114.0 3.1 %collective-permute-done.10.far_top = bf16[256,512]{1,0:T(8,128)(2,1)S(1)} collective-permute-done((bf16[256,512]{1,0:T(8,128)(2,1)}, bf16[256,512]{1,0:T(8,128)(2,1)S(1)}, u32[]{:S(2)}, u32[]{:S(2)}) %collective-permute-start.10) | collective-permute-done | bytes 262176 | tf_op jit(solution)/shard_map/ppermute | solution.py:23
  117.7 11.1 %feed_forward.1 = (bf16[512,512]{1,0:T(8,128)(2,1)}, bf16[512,512]{1,0:T(8,128)(2,1)}, bf16[512,512]{1,0:T(8,128)(2,1)}, bf16[256,512]{1,0:T(8,128)(2,1)}, bf16[256,512]{1,0:T(8,128)(2,1)}) custom-call(bf16[512,512]{1,0:T(8,128)(2,1)} %copy-done.2, bf16[512,512]{1,0:T(8,128)(2,1)} %copy-done.7, bf16[512,512]{1,0:T(8,128)(2,1)} %copy-done.8, ...), custom_call_target="tpu_custom_call" | custom-call | tf_op jit(solution)/shard_map/feed_forward/pallas_call | solution.py:283
  129.0 3.4 %collective-permute-start.12 = (bf16[512,512]{1,0:T(8,128)(2,1)}, bf16[512,512]{1,0:T(8,128)(2,1)}, u32[]{:S(2)}, u32[]{:S(2)}) collective-permute-start(bf16[512,512]{1,0:T(8,128)(2,1)} %get-tuple-element.32), channel_id=1, source_target_pairs={{0,3},{1,0},{2,1},{3,2},{4,7},{5,4},{6,5},{7,6},{8,11},{9,8},{10,9... | collective-permute-start | bytes 1572872 | tf_op jit(solution)/shard_map/ppermute | solution.py:23
  132.4 9.9 %collective-permute-done.13 = bf16[512,512]{1,0:T(8,128)(2,1)S(1)} collective-permute-done((bf16[512,512]{1,0:T(8,128)(2,1)}, bf16[512,512]{1,0:T(8,128)(2,1)S(1)}, u32[]{:S(2)}, u32[]{:S(2)}) %collective-permute-start.13) | collective-permute-done | bytes 524320 | tf_op jit(solution)/shard_map/ppermute | solution.py:23
  142.3 1.9 %add_convert_fusion.1 = bf16[256,512]{1,0:T(8,128)(2,1)} fusion(bf16[256,512]{1,0:T(8,128)(2,1)} %get-tuple-element.33, bf16[512,512]{1,0:T(8,128)(2,1)S(1)} %collective-permute-done.13), kind=kLoop, calls=%fused_computation.8 | loop fusion | flops 524288 | bytes 786432 | tf_op jit(solution)/shard_map/convert_element_type | solution.py:46
  144.3 1.6 copy-done
  145.9 3.3 %reorder.1 = bf16[32,2,16,2,256]{4,3,2,1,0:T(2,128)(2,1)} custom-call(s32[32]{0:T(128)} %slot_map.5, bf16[32,96,2,256]{3,2,1,0:T(2,128)(2,1)} %copy-done), custom_call_target="tpu_custom_call" | custom-call | tf_op jit(solution)/shard_map/reorder/pallas_call | solution.py:412
  149.2 7.1 %all-to-all-start.2 = ((bf16[32,2,16,2,256]{4,3,2,1,0:T(2,128)(2,1)}), bf16[32,2,16,2,256]{4,3,2,1,0:T(2,128)(2,1)S(1)}, u32[]{:S(2)}, u32[]{:S(2)}) async-start(bf16[32,2,16,2,256]{4,3,2,1,0:T(2,128)(2,1)} %reorder.1), calls=%async_computation.2 | async-start | bytes 2097152 | tf_op jit(solution)/shard_map/all_to_all | solution.py:508
  157.3 3.3 %collective-permute-start.15 = (bf16[256,512]{1,0:T(8,128)(2,1)S(1)}, bf16[256,512]{1,0:T(8,128)(2,1)S(1)}, u32[]{:S(2)}, u32[]{:S(2)}) collective-permute-start(bf16[256,512]{1,0:T(8,128)(2,1)S(1)} %add_convert_fusion), channel_id=1, source_target_pairs={{0,3},{1,0},{2,1},{3,2},{4,7},{5,4},{6,5},{7,6},{8,11},{9,8},{10,9... | collective-permute-start | bytes 786440 | tf_op jit(solution)/shard_map/ppermute | solution.py:23
  161.4 5.2 %collective-permute-done.15 = bf16[256,512]{1,0:T(8,128)(2,1)S(1)} collective-permute-done((bf16[256,512]{1,0:T(8,128)(2,1)S(1)}, bf16[256,512]{1,0:T(8,128)(2,1)S(1)}, u32[]{:S(2)}, u32[]{:S(2)}) %collective-permute-start.15) | collective-permute-done | bytes 262176 | tf_op jit(solution)/shard_map/ppermute | solution.py:23
  166.6 1.3 convert_add_fusion.1
  168.9 4.6 %all-to-all-done.2.new = bf16[32,2,16,2,256]{4,3,2,1,0:T(2,128)(2,1)S(1)} async-done(((bf16[32,2,16,2,256]{4,3,2,1,0:T(2,128)(2,1)}), bf16[32,2,16,2,256]{4,3,2,1,0:T(2,128)(2,1)S(1)}, u32[]{:S(2)}, u32[]{:S(2)}) %all-to-all-start.2) | async-done | bytes 1048608 | tf_op jit(solution)/shard_map/all_to_all | solution.py:508
  174.5 5.1 %pages.1 = bf16[1,12,256,2,256]{4,3,2,1,0:T(2,128)(2,1)} custom-call(s32[32]{0:T(128)} %slot_map.5, s32[32]{0:T(128)} %prior_len.1, s32[192]{0:T(256)} %reshape.56.table, bf16[32,96,2,256]{3,2,1,0:T(2,128)(2,1)} %copy-done, bf16[32,2,16,2,256]{4,3,2,1,0:T(2,128)(2,1)} %copy-done.4), custom_call_target="tpu_custom_call" | custom-call | tf_op jit(solution)/shard_map/pages/pallas_call | solution.py:476
  (83 shorter events, 15.3 us)
Async XLA Ops:
  0.6 11.8 %copy-start.22 = (s32[32]{0:T(128)S(1)}, s32[32]{0:T(128)}, u32[]{:S(2)}) copy-start(s32[32]{0:T(128)} %prior_len.1) | copy-start | bytes 388
  0.7 28.3 %copy-start.17 = (f32[2048]{0:T(1024)S(1)}, f32[2048]{0:T(1024)}, u32[]{:S(2)}) copy-start(f32[2048]{0:T(1024)} %param.15) | copy-start | bytes 24580
  0.7 28.9 %copy-start.18 = (f32[2048]{0:T(1024)S(1)}, f32[2048]{0:T(1024)}, u32[]{:S(2)}) copy-start(f32[2048]{0:T(1024)} %param.16) | copy-start | bytes 24580
  0.7 65.1 %all-to-all-start = ((bf16[32,32,2,512]{3,2,1,0:T(2,128)(2,1)}), bf16[32,32,2,512]{3,2,1,0:T(2,128)(2,1)S(1)}, u32[]{:S(2)}, u32[]{:S(2)}) async-start(bf16[32,32,2,512]{3,2,1,0:T(2,128)(2,1)} %bitcast.8), calls=%async_computation | async-start | bytes 4194304 | tf_op jit(solution)/shard_map/all_to_all | solution.py:508
  9.1 15.4 %collective-permute-start = (bf16[512,512]{1,0:T(8,128)(2,1)S(1)}, bf16[512,512]{1,0:T(8,128)(2,1)S(1)}, u32[]{:S(2)}, u32[]{:S(2)}) collective-permute-start(bf16[512,512]{1,0:T(8,128)(2,1)S(1)} %copy-done.5), channel_id=1, source_target_pairs={{0,1},{1,2},{2,3},{3,0},{4,5},{5,6},{6,7},{7,4},{8,9},{9,10},{10,1... | collective-permute-start | bytes 1572872 | tf_op jit(solution)/shard_map/ppermute | solution.py:23
  10.8 14.2 %collective-permute-start.1 = (bf16[512,512]{1,0:T(8,128)(2,1)S(1)}, bf16[512,512]{1,0:T(8,128)(2,1)}, u32[]{:S(2)}, u32[]{:S(2)}) collective-permute-start(bf16[512,512]{1,0:T(8,128)(2,1)S(1)} %copy-done.5), channel_id=1, source_target_pairs={{0,3},{1,0},{2,1},{3,2},{4,7},{5,4},{6,5},{7,6},{8,11},{9,8},{10,9... | collective-permute-start | bytes 1572872 | tf_op jit(solution)/shard_map/ppermute | solution.py:23
  24.6 12.3 %copy-start.9 = (bf16[512,512]{1,0:T(8,128)(2,1)}, bf16[512,512]{1,0:T(8,128)(2,1)S(1)}, u32[]{:S(2)}) copy-start(bf16[512,512]{1,0:T(8,128)(2,1)S(1)} %collective-permute-done.left) | copy-start | bytes 1572868
  24.6 12.3 %collective-permute-start.2 = (bf16[256,512]{1,0:T(8,128)(2,1)S(1)}, bf16[256,512]{1,0:T(8,128)(2,1)}, u32[]{:S(2)}, u32[]{:S(2)}) collective-permute-start(bf16[256,512]{1,0:T(8,128)(2,1)S(1)} %slice.64), channel_id=1, source_target_pairs={{0,1},{1,2},{2,3},{3,0},{4,5},{5,6},{6,7},{7,4},{8,9},{9,10},{10,1... | collective-permute-start | bytes 786440 | tf_op jit(solution)/shard_map/ppermute | solution.py:23
  25.9 10.9 %collective-permute-start.3 = (bf16[256,512]{1,0:T(8,128)(2,1)S(1)}, bf16[256,512]{1,0:T(8,128)(2,1)S(1)}, u32[]{:S(2)}, u32[]{:S(2)}) collective-permute-start(bf16[256,512]{1,0:T(8,128)(2,1)S(1)} %slice.65), channel_id=1, source_target_pairs={{0,3},{1,0},{2,1},{3,2},{4,7},{5,4},{6,5},{7,6},{8,11},{9,8},{10,9... | collective-permute-start | bytes 786440 | tf_op jit(solution)/shard_map/ppermute | solution.py:23
  62.5 17.1 %collective-permute-start.5 = (bf16[512,512]{1,0:T(8,128)(2,1)}, bf16[512,512]{1,0:T(8,128)(2,1)}, u32[]{:S(2)}, u32[]{:S(2)}) collective-permute-start(bf16[512,512]{1,0:T(8,128)(2,1)} %get-tuple-element.27), channel_id=1, source_target_pairs={{0,1},{1,2},{2,3},{3,0},{4,5},{5,6},{6,7},{7,4},{8,9},{9,10},{10,1... | collective-permute-start | bytes 1572872 | tf_op jit(solution)/shard_map/ppermute | solution.py:23
  62.6 18.2 %collective-permute-start.4 = (bf16[512,512]{1,0:T(8,128)(2,1)}, bf16[512,512]{1,0:T(8,128)(2,1)}, u32[]{:S(2)}, u32[]{:S(2)}) collective-permute-start(bf16[512,512]{1,0:T(8,128)(2,1)} %get-tuple-element.25), channel_id=1, source_target_pairs={{0,3},{1,0},{2,1},{3,2},{4,7},{5,4},{6,5},{7,6},{8,11},{9,8},{10,9... | collective-permute-start | bytes 1572872 | tf_op jit(solution)/shard_map/ppermute | solution.py:23
  72.1 8.6 %copy-start.14 = (bf16[256,512]{1,0:T(8,128)(2,1)S(1)}, bf16[256,512]{1,0:T(8,128)(2,1)}, u32[]{:S(2)}) copy-start(bf16[256,512]{1,0:T(8,128)(2,1)} %get-tuple-element.28) | copy-start | bytes 786436
  72.1 72.1 %all-to-all-start.1 = ((bf16[32,96,2,256]{3,2,1,0:T(2,128)(2,1)}), bf16[32,96,2,256]{3,2,1,0:T(2,128)(2,1)S(1)}, u32[]{:S(2)}, u32[]{:S(2)}) async-start(bf16[32,96,2,256]{3,2,1,0:T(2,128)(2,1)} %mix.1), calls=%async_computation.1 | async-start | bytes 6291456 | tf_op jit(solution)/shard_map/all_to_all | solution.py:508
  80.6 10.9 %collective-permute-start.6 = (bf16[256,512]{1,0:T(8,128)(2,1)S(1)}, bf16[256,512]{1,0:T(8,128)(2,1)S(1)}, u32[]{:S(2)}, u32[]{:S(2)}) collective-permute-start(bf16[256,512]{1,0:T(8,128)(2,1)S(1)} %add_convert_fusion.3), channel_id=1, source_target_pairs={{0,1},{1,2},{2,3},{3,0},{4,5},{5,6},{6,7},{7,4},{8,9},{9,10},{10,1... | collective-permute-start | bytes 786440 | tf_op jit(solution)/shard_map/ppermute | solution.py:23
  81.8 9.8 %copy-start.11 = (bf16[512,512]{1,0:T(8,128)(2,1)S(1)}, bf16[512,512]{1,0:T(8,128)(2,1)}, u32[]{:S(2)}) copy-start(bf16[512,512]{1,0:T(8,128)(2,1)} %get-tuple-element.24) | copy-start | bytes 1572868
  81.8 11.0 %copy-start.6 = (bf16[512,512]{1,0:T(8,128)(2,1)S(1)}, bf16[512,512]{1,0:T(8,128)(2,1)}, u32[]{:S(2)}) copy-start(bf16[512,512]{1,0:T(8,128)(2,1)} %own.1) | copy-start | bytes 1572868
  81.8 9.7 %collective-permute-start.7 = (bf16[256,512]{1,0:T(8,128)(2,1)S(1)}, bf16[256,512]{1,0:T(8,128)(2,1)S(1)}, u32[]{:S(2)}, u32[]{:S(2)}) collective-permute-start(bf16[256,512]{1,0:T(8,128)(2,1)S(1)} %add_convert_fusion.2), channel_id=1, source_target_pairs={{0,3},{1,0},{2,1},{3,2},{4,7},{5,4},{6,5},{7,6},{8,11},{9,8},{10,9... | collective-permute-start | bytes 786440 | tf_op jit(solution)/shard_map/ppermute | solution.py:23
  91.5 21.2 %copy-start.19 = (f32[2048]{0:T(1024)S(1)}, f32[2048]{0:T(1024)}, u32[]{:S(2)}) copy-start(f32[2048]{0:T(1024)} %param.20) | copy-start | bytes 24580
  91.5 21.8 %copy-start.20 = (f32[2048]{0:T(1024)S(1)}, f32[2048]{0:T(1024)}, u32[]{:S(2)}) copy-start(f32[2048]{0:T(1024)} %param.21) | copy-start | bytes 24580
  93.0 14.8 %collective-permute-start.8 = (bf16[512,512]{1,0:T(8,128)(2,1)S(1)}, bf16[512,512]{1,0:T(8,128)(2,1)S(1)}, u32[]{:S(2)}, u32[]{:S(2)}) collective-permute-start(bf16[512,512]{1,0:T(8,128)(2,1)S(1)} %fusion.own), channel_id=1, source_target_pairs={{0,1},{1,2},{2,3},{3,0},{4,5},{5,6},{6,7},{7,4},{8,9},{9,10},{10,1... | collective-permute-start | bytes 1572872 | tf_op jit(solution)/shard_map/ppermute | solution.py:23
  93.7 14.8 %collective-permute-start.9 = (bf16[512,512]{1,0:T(8,128)(2,1)S(1)}, bf16[512,512]{1,0:T(8,128)(2,1)S(1)}, u32[]{:S(2)}, u32[]{:S(2)}) collective-permute-start(bf16[512,512]{1,0:T(8,128)(2,1)S(1)} %fusion.own), channel_id=1, source_target_pairs={{0,3},{1,0},{2,1},{3,2},{4,7},{5,4},{6,5},{7,6},{8,11},{9,8},{10,9... | collective-permute-start | bytes 1572872 | tf_op jit(solution)/shard_map/ppermute | solution.py:23
  108.6 8.5 %collective-permute-start.10 = (bf16[256,512]{1,0:T(8,128)(2,1)}, bf16[256,512]{1,0:T(8,128)(2,1)S(1)}, u32[]{:S(2)}, u32[]{:S(2)}) collective-permute-start(bf16[256,512]{1,0:T(8,128)(2,1)} %slice.70), channel_id=1, source_target_pairs={{0,1},{1,2},{2,3},{3,0},{4,5},{5,6},{6,7},{7,4},{8,9},{9,10},{10,1... | collective-permute-start | bytes 786440 | tf_op jit(solution)/shard_map/ppermute | solution.py:23
  109.6 7.7 %collective-permute-start.11 = (bf16[256,512]{1,0:T(8,128)(2,1)}, bf16[256,512]{1,0:T(8,128)(2,1)}, u32[]{:S(2)}, u32[]{:S(2)}) collective-permute-start(bf16[256,512]{1,0:T(8,128)(2,1)} %slice.71), channel_id=1, source_target_pairs={{0,3},{1,0},{2,1},{3,2},{4,7},{5,4},{6,5},{7,6},{8,11},{9,8},{10,9... | collective-permute-start | bytes 786440 | tf_op jit(solution)/shard_map/ppermute | solution.py:23
  128.9 13.4 %collective-permute-start.13 = (bf16[512,512]{1,0:T(8,128)(2,1)}, bf16[512,512]{1,0:T(8,128)(2,1)S(1)}, u32[]{:S(2)}, u32[]{:S(2)}) collective-permute-start(bf16[512,512]{1,0:T(8,128)(2,1)} %get-tuple-element.34), channel_id=1, source_target_pairs={{0,1},{1,2},{2,3},{3,0},{4,5},{5,6},{6,7},{7,4},{8,9},{9,10},{10,1... | collective-permute-start | bytes 1572872 | tf_op jit(solution)/shard_map/ppermute | solution.py:23
  129.0 27.3 %collective-permute-start.12 = (bf16[512,512]{1,0:T(8,128)(2,1)}, bf16[512,512]{1,0:T(8,128)(2,1)}, u32[]{:S(2)}, u32[]{:S(2)}) collective-permute-start(bf16[512,512]{1,0:T(8,128)(2,1)} %get-tuple-element.32), channel_id=1, source_target_pairs={{0,3},{1,0},{2,1},{3,2},{4,7},{5,4},{6,5},{7,6},{8,11},{9,8},{10,9... | collective-permute-start | bytes 1572872 | tf_op jit(solution)/shard_map/ppermute | solution.py:23
  144.2 12.1 %copy-start.13 = (bf16[256,512]{1,0:T(8,128)(2,1)S(1)}, bf16[256,512]{1,0:T(8,128)(2,1)}, u32[]{:S(2)}) copy-start(bf16[256,512]{1,0:T(8,128)(2,1)} %get-tuple-element.35) | copy-start | bytes 786436
  144.2 16.4 %copy-start.21 = (s32[32,6]{0,1:T(8,128)S(1)}, s32[32,6]{0,1:T(8,128)}, u32[]{:S(2)}) copy-start(s32[32,6]{0,1:T(8,128)} %param.27) | copy-start | bytes 2308
  144.2 17.2 %collective-permute-start.14 = (bf16[256,512]{1,0:T(8,128)(2,1)}, bf16[256,512]{1,0:T(8,128)(2,1)}, u32[]{:S(2)}, u32[]{:S(2)}) collective-permute-start(bf16[256,512]{1,0:T(8,128)(2,1)} %add_convert_fusion.1), channel_id=1, source_target_pairs={{0,1},{1,2},{2,3},{3,0},{4,5},{5,6},{6,7},{7,4},{8,9},{9,10},{10,1... | collective-permute-start | bytes 786440 | tf_op jit(solution)/shard_map/ppermute | solution.py:23
  149.2 17.4 %copy-start.10 = (bf16[512,512]{1,0:T(8,128)(2,1)S(1)}, bf16[512,512]{1,0:T(8,128)(2,1)}, u32[]{:S(2)}) copy-start(bf16[512,512]{1,0:T(8,128)(2,1)} %get-tuple-element.31) | copy-start | bytes 1572868
  149.2 18.7 %copy-start.3 = (bf16[512,512]{1,0:T(8,128)(2,1)S(1)}, bf16[512,512]{1,0:T(8,128)(2,1)}, u32[]{:S(2)}) copy-start(bf16[512,512]{1,0:T(8,128)(2,1)} %copy-done.2) | copy-start | bytes 1572868
  149.2 24.3 %all-to-all-start.2 = ((bf16[32,2,16,2,256]{4,3,2,1,0:T(2,128)(2,1)}), bf16[32,2,16,2,256]{4,3,2,1,0:T(2,128)(2,1)S(1)}, u32[]{:S(2)}, u32[]{:S(2)}) async-start(bf16[32,2,16,2,256]{4,3,2,1,0:T(2,128)(2,1)} %reorder.1), calls=%async_computation.2 | async-start | bytes 2097152 | tf_op jit(solution)/shard_map/all_to_all | solution.py:508
  157.3 9.3 %collective-permute-start.15 = (bf16[256,512]{1,0:T(8,128)(2,1)S(1)}, bf16[256,512]{1,0:T(8,128)(2,1)S(1)}, u32[]{:S(2)}, u32[]{:S(2)}) collective-permute-start(bf16[256,512]{1,0:T(8,128)(2,1)S(1)} %add_convert_fusion), channel_id=1, source_target_pairs={{0,3},{1,0},{2,1},{3,2},{4,7},{5,4},{6,5},{7,6},{8,11},{9,8},{10,9... | collective-permute-start | bytes 786440 | tf_op jit(solution)/shard_map/ppermute | solution.py:23
  (10 other events, 18.4 us)

commit v2 on v0

--- a/solution.py
+++ b/solution.py
@@ -17,6 +17,7 @@
 
 
 OFFSETS = (0, 3, 1, 2)
+EARLY = 8
 
 
 def shift_by(value, step):
@@ -311,23 +312,29 @@
     lax.fori_loop(0, slot_map.shape[0], body, 0)
 
 
-def mix_kernel(slot_map, pieces, keys, values, out, owners, stage, sems):
-    count, rows, _, width = pieces.shape
-    half = width // 2
-    fresh = keys.shape[0] // count
-    find_owners(slot_map, owners)
+def send_old(pieces, owners, out, sem, first, rows):
+    half = pieces.shape[3] // 2
 
     def send(slot, carry):
         group = slot // 2
         for side in range(2):
             pltpu.make_async_copy(
-                pieces.at[owners[slot], :, :, side * half : (side + 1) * half],
+                pieces.at[owners[slot], pl.ds(first, rows), :, side * half : (side + 1) * half],
                 out.at[2 * group + side, pl.ds((slot - 2 * group) * rows, rows)],
-                sems.at[0],
+                sem,
             ).start()
         return carry
 
-    lax.fori_loop(0, count, send, 0)
+    lax.fori_loop(0, pieces.shape[0], send, 0)
+
+
+def mix_kernel(slot_map, pieces, keys, values, out, owners, stage, sems):
+    count = pieces.shape[0]
+    half = pieces.shape[3] // 2
+    fresh = keys.shape[0] // count
+    early = out.shape[1] // 2 - fresh
+    find_owners(slot_map, owners)
+    send_old(pieces, owners, out, sems.at[0], 0, early)
 
     def weave(slot, carry):
         at = pl.multiple_of(slot * fresh, fresh)
@@ -338,19 +345,19 @@
         return carry
 
     lax.fori_loop(0, count, weave, 0)
-    last = pltpu.make_async_copy(stage, out.at[:, 2 * rows :], sems.at[1])
+    last = pltpu.make_async_copy(stage, out.at[:, 2 * early :], sems.at[1])
     last.start()
-    first = out.at[:, : 2 * rows]
+    first = out.at[:, : 2 * early]
     pltpu.make_async_copy(first, first, sems.at[0]).wait()
     last.wait()
 
 
-def mix(slot_map, pieces, keys, values):
-    count, rows, _, width = pieces.shape
+def mix(slot_map, pieces, keys, values, early):
+    count, _, _, width = pieces.shape
     fresh = keys.shape[0] // count
     return pl.pallas_call(
         mix_kernel,
-        out_shape=jax.ShapeDtypeStruct((count, 2 * rows + 2 * fresh, 2, width // 2), BF),
+        out_shape=jax.ShapeDtypeStruct((count, 2 * early + 2 * fresh, 2, width // 2), BF),
         in_specs=specs("s", "v", "v", "v"),
         out_specs=specs("a")[0],
         scratch_shapes=[
@@ -363,50 +370,74 @@
     )(slot_map, pieces, keys, values)
 
 
-def reorder_kernel(slot_map, mixed, out, owners, sem):
-    count, rows, _, _ = mixed.shape
-    fresh = out.shape[2]
+def reorder_kernel(slot_map, pieces, mixed, out, owners, stage, sems):
+    count, rows, _, _ = pieces.shape
+    fresh = stage.shape[1] // 2
+    late = out.shape[1] // 2 - fresh
+    early = rows - late
     find_owners(slot_map, owners)
+
+    def load(slot, carry):
+        pltpu.make_async_copy(mixed.at[owners[slot], pl.ds(2 * early, 2 * fresh)], stage.at[slot], sems.at[0]).start()
+        return carry
+
+    lax.fori_loop(0, count, load, 0)
+    send_old(pieces, owners, out, sems.at[1], early, late)
+    pltpu.make_async_copy(stage, stage, sems.at[0]).wait()
 
     def send(slot, carry):
         group = slot // 2
         for side in range(2):
             pltpu.make_async_copy(
-                mixed.at[owners[slot], pl.ds(rows - (2 - side) * fresh, fresh)],
-                out.at[2 * group + side, slot - 2 * group],
-                sem,
+                stage.at[slot, pl.ds(side * fresh, fresh)],
+                out.at[2 * group + side, pl.ds(2 * late + (slot - 2 * group) * fresh, fresh)],
+                sems.at[2],
             ).start()
         return carry
 
     lax.fori_loop(0, count, send, 0)
-    pltpu.make_async_copy(out, out, sem).wait()
-
-
-def reorder(slot_map, mixed, fresh):
-    count, _, _, width = mixed.shape
+    first, last = out.at[:, : 2 * late], out.at[:, 2 * late :]
+    pltpu.make_async_copy(first, first, sems.at[1]).wait()
+    pltpu.make_async_copy(last, last, sems.at[2]).wait()
+
+
+def reorder(slot_map, pieces, mixed, fresh):
+    count, rows, _, width = pieces.shape
+    late = rows - (mixed.shape[1] // 2 - fresh)
     return pl.pallas_call(
         reorder_kernel,
-        out_shape=jax.ShapeDtypeStruct((count, 2, fresh, 2, width), BF),
-        in_specs=specs("s", "a"),
-        out_specs=specs("v")[0],
-        scratch_shapes=[pltpu.SMEM((count,), jnp.int32), pltpu.SemaphoreType.DMA],
+        out_shape=jax.ShapeDtypeStruct((count, 2 * late + 2 * fresh, 2, width // 2), BF),
+        in_specs=specs("s", "v", "a"),
+        out_specs=specs("a")[0],
+        scratch_shapes=[
+            pltpu.SMEM((count,), jnp.int32),
+            pltpu.VMEM((count, 2 * fresh, 2, width // 2), BF),
+            pltpu.SemaphoreType.DMA((3,)),
+        ],
         compiler_params=PARAMS,
         name="reorder",
-    )(slot_map, mixed)
-
-
-def pages_kernel(slot_map, prior_len, table, mixed, new, out, owners, full, blank, sems):
-    count, _, new_rows, _, _ = new.shape
-    old_rows = (mixed.shape[1] - 2 * new_rows) // 2
+    )(slot_map, pieces, mixed)
+
+
+def pages_kernel(slot_map, prior_len, table, mixed, rest, out, owners, full, blank, sems):
+    count = mixed.shape[0]
+    blocks = out.shape[1] // 2
+    new_rows = (mixed.shape[1] + rest.shape[1]) // 2 - blocks * BLOCK // count
+    early = mixed.shape[1] // 2 - new_rows
+    late = rest.shape[1] // 2 - new_rows
+    old_rows = early + late
     cached, fresh = count * old_rows, count * new_rows
-    blocks = (cached + fresh) // BLOCK
     group = lax.axis_index("req") // 2
     find_owners(slot_map, owners)
     for slot in range(2):
 
         def load(index, carry, slot=slot):
-            pltpu.make_async_copy(
-                mixed.at[index, pl.ds(slot * old_rows, old_rows)], full.at[slot, pl.ds(index * old_rows, old_rows)], sems.at[0, slot]
+            if early:
+                pltpu.make_async_copy(
+                    mixed.at[index, pl.ds(slot * early, early)], full.at[slot, pl.ds(index * old_rows, early)], sems.at[0, slot]
+                ).start()
+            pltpu.make_async_copy(
+                rest.at[index, pl.ds(slot * late, late)], full.at[slot, pl.ds(index * old_rows + early, late)], sems.at[0, slot]
             ).start()
             return carry
 
@@ -427,7 +458,9 @@
 
         def store(index, carry, slot=slot, length=length):
             pltpu.make_async_copy(
-                new.at[index, slot], full.at[slot, pl.ds(length + index * new_rows, new_rows)], sems.at[1, slot]
+                rest.at[index, pl.ds(2 * late + slot * new_rows, new_rows)],
+                full.at[slot, pl.ds(length + index * new_rows, new_rows)],
+                sems.at[1, slot],
             ).start()
             return carry
 
@@ -444,10 +477,10 @@
     pltpu.make_async_copy(out, out, sems.at[2, 0]).wait()
 
 
-def pages(slot_map, prior_len, table, mixed, new):
-    count, _, new_rows, _, width = new.shape
-    cached = count * (mixed.shape[1] - 2 * new_rows) // 2
-    fresh = count * new_rows
+def pages(slot_map, prior_len, table, mixed, rest, fresh):
+    count, _, _, width = mixed.shape
+    cached = count * (mixed.shape[1] + rest.shape[1] - 4 * fresh) // 2
+    fresh = count * fresh
     return pl.pallas_call(
         pages_kernel,
         out_shape=jax.ShapeDtypeStruct((1, 2 * (cached + fresh) // BLOCK, BLOCK, 2, width), BF),
@@ -461,7 +494,7 @@
         ],
         compiler_params=PARAMS,
         name="pages",
-    )(slot_map, prior_len, table, mixed, new)
+    )(slot_map, prior_len, table, mixed, rest)
 
 
 def rotary_tables(prior_count, rows):
@@ -518,26 +551,22 @@
         tables,
     )
     parts = attend(prior_len, queries, new_keys, new_values, old_keys, old_values, output_weight)
-    mixed = mix(slot_map, old, new_keys, new_values)
+    mixed = mix(slot_map, old, new_keys, new_values, EARLY)
     mixed = exchange(mixed)
     top_sum, bottom_sum = ring_scatter(parts)
     top = (top.astype(F32) + top_sum).astype(BF)
     bottom = (bottom.astype(F32) + bottom_sum).astype(BF)
+    expand = jnp.transpose(expand_weight, (1, 0, 2))
+    top, bottom, expand = lax.optimization_barrier((top, bottom, expand))
     pieces = ring_gather(top, bottom)
-    parts = feed_forward(
-        pieces,
-        second_gain.reshape(4, width),
-        second_shift.reshape(4, width),
-        jnp.transpose(expand_weight, (1, 0, 2)),
-        contract_weight,
-    )
-    new = reorder(slot_map, mixed, rows // count)
-    new = exchange(new)
+    parts = feed_forward(pieces, second_gain.reshape(4, width), second_shift.reshape(4, width), expand, contract_weight)
+    rest = reorder(slot_map, old, mixed, rows // count)
+    rest = exchange(rest)
     top_sum, bottom_sum = ring_scatter(parts)
     result = jnp.concatenate(
         [(top.astype(F32) + top_sum).astype(BF), (bottom.astype(F32) + bottom_sum).astype(BF)], axis=0
     )
-    page_pool = pages(slot_map, prior_len, block_table.reshape(-1), mixed, new)
+    page_pool = pages(slot_map, prior_len, block_table.reshape(-1), mixed, rest, rows // count)
     return (result, page_pool)
 
 

time: 172 us -> 179 us (1.041)
  waiting for transfers between devices: 29.6 us -> 33 us
  other arithmetic: 10.9 us -> 13.3 us
    ppermute x24, waiting for transfers between devices: 29.5 us -> 33 us  [shift_by(): return lax.ppermute(value, 'tp', [(i, (i + step) % 4) for i in range(4)])]
    unnamed x42 -> x52, local copies, waits for them, and re-layouts: 10.4 us -> 10.6 us
  transfers between devices with their start and end apart: 27 -> 27, of which waited for: 10 -> 12; matrix products, arithmetic and copies ran while one was open for 12% -> 13% of each run, Pallas kernels for 26% -> 25%
where the time goes in v2:
time: 179 us; the launch traced here: 178 us
  starting transfers between devices  60.7 us (34%)
  Pallas kernels  55.5 us (31%)
  waiting for transfers between devices  33 us (18%)
  local copies, waits for them, and re-layouts  14.3 us (8%)
  other arithmetic  13.3 us (7%)
    ppermute x24, starting transfers between devices, shift_by(): return lax.ppermute(value, 'tp', [(i, (i + step) % 4) for i in range(4)])  37.5 us
    ppermute x24, waiting for transfers between devices, shift_by(): return lax.ppermute(value, 'tp', [(i, (i + step) % 4) for i in range(4)])  33 us
    all_to_all x3, starting transfers between devices, exchange(): lax.all_to_all(pieces, 'req', split_axis=0, concat_axis=0, tiled=True)  23.2 us
    pallas_call x1, Pallas kernels, attend(): pl.pallas_call(attend_kernel, out_shape=(jax.ShapeDtypeStruct((rows // 2,...  16.1 us
    pallas_call x1, Pallas kernels, feed_forward(): pl.pallas_call(forward_kernel, out_shape=(jax.ShapeDtypeStruct((half, wid...  11 us
    unnamed x52, local copies, waits for them, and re-layouts  10.6 us
    pallas_call x1, Pallas kernels, project(): pl.pallas_call(project_kernel, out_shape=(out, out, out), in_specs=specs(...  8.85 us
    pallas_call x1, Pallas kernels, pages(): pl.pallas_call(pages_kernel, out_shape=jax.ShapeDtypeStruct((1, 2 * (cach...  5.1 us
  transfers between devices with their start and end apart: 27, of which 12 were waited for; matrix products, arithmetic and copies ran while one was open for 13% of the time, Pallas kernels for 25%

profile of v2, /device:TPU:0, one launch (start us, length us, event | category | flops | bytes accessed | tf_op | source)
XLA Modules:
  0.0 177.9 jit_solution(9421198372177198462)
XLA Ops:
  0.7 8.4 %all-to-all-start = ((bf16[32,32,2,512]{3,2,1,0:T(2,128)(2,1)}), bf16[32,32,2,512]{3,2,1,0:T(2,128)(2,1)S(1)}, u32[]{:S(2)}, u32[]{:S(2)}) async-start(bf16[32,32,2,512]{3,2,1,0:T(2,128)(2,1)} %bitcast.8), calls=%async_computation | async-start | bytes 4194304 | tf_op jit(solution)/shard_map/all_to_all | solution.py:516
  12.8 2.9 %collective-permute-start.2 = (bf16[256,512]{1,0:T(8,128)(2,1)S(1)}, bf16[256,512]{1,0:T(8,128)(2,1)}, u32[]{:S(2)}, u32[]{:S(2)}) collective-permute-start(bf16[256,512]{1,0:T(8,128)(2,1)S(1)} %get-tuple-element.53.o0), channel_id=1, source_target_pairs={{0,3},{1,0},{2,1},{3,2},{4,7},{5,4},{6,5},{7,6},{8,11},{9,8},{10,9... | collective-permute-start | bytes 786440 | tf_op jit(solution)/shard_map/ppermute | solution.py:24
  17.0 2.7 %collective-permute-done.l0 = bf16[256,512]{1,0:T(8,128)(2,1)S(1)} collective-permute-done((bf16[256,512]{1,0:T(8,128)(2,1)S(1)}, bf16[256,512]{1,0:T(8,128)(2,1)S(1)}, u32[]{:S(2)}, u32[]{:S(2)}) %collective-permute-start) | collective-permute-done | bytes 262176 | tf_op jit(solution)/shard_map/ppermute | solution.py:24
  20.0 2.9 %collective-permute-start.5 = (bf16[256,512]{1,0:T(8,128)(2,1)S(1)}, bf16[256,512]{1,0:T(8,128)(2,1)}, u32[]{:S(2)}, u32[]{:S(2)}) collective-permute-start(bf16[256,512]{1,0:T(8,128)(2,1)S(1)} %collective-permute-done.3.r1), channel_id=1, source_target_pairs={{0,3},{1,0},{2,1},{3,2},{4,7},{5,4},{6,5},{7,6},{8,11},{9,8},{10,9... | collective-permute-start | bytes 786440 | tf_op jit(solution)/shard_map/ppermute | solution.py:24
  24.1 1.9 %fusion = (f32[512,128]{1,0:T(8,128)}, f32[512,128]{1,0:T(8,128)}, f32[512,128]{1,0:T(8,128)}) fusion(f32[128]{0:T(128)S(1)} %compare_select_fusion.2, f32[512]{0:T(512)S(1)} %add_convert_fusion.8, pred[128]{0:T(512)(128)(4,1)S(1)} %get-tuple-element.57, pred[128]{0:T(512)(128)(4,1)S(1)} %get-tuple-element.58), kind=kLoop, calls=%fused_computation.12 | loop fusion | flops 262144 | bytes 789248 | tf_op jit(solution)/shard_map/jit(_where)/select_n | solution.py:511
  26.0 4.4 %collective-permute-done.4.f0 = bf16[256,512]{1,0:T(8,128)(2,1)} collective-permute-done((bf16[256,512]{1,0:T(8,128)(2,1)S(1)}, bf16[256,512]{1,0:T(8,128)(2,1)}, u32[]{:S(2)}, u32[]{:S(2)}) %collective-permute-start.4) | collective-permute-done | bytes 262176 | tf_op jit(solution)/shard_map/ppermute | solution.py:24
  30.4 8.9 %project.1 = (bf16[512,512]{1,0:T(8,128)(2,1)}, bf16[512,512]{1,0:T(8,128)(2,1)}, bf16[512,512]{1,0:T(8,128)(2,1)}) custom-call(bf16[256,512]{1,0:T(8,128)(2,1)} %copy-done.9, bf16[256,512]{1,0:T(8,128)(2,1)} %copy-done.8, bf16[256,512]{1,0:T(8,128)(2,1)} %copy-done.16, bf16[256,512]{1,0:T(8,128)(2,1)} %copy-done.18, ...), custom_call_target="tpu_custom_call" | custom-call | tf_op jit(solution)/shard_map/project/pallas_call | solution.py:129
  40.6 5.0 %mix.1 = bf16[32,48,2,256]{3,2,1,0:T(2,128)(2,1)} custom-call(s32[32]{0:T(128)} %slot_map.5, bf16[32,32,2,512]{3,2,1,0:T(2,128)(2,1)} %copy-done, bf16[512,512]{1,0:T(8,128)(2,1)} %get-tuple-element.27.new_keys.keys, bf16[512,512]{1,0:T(8,128)(2,1)} %get-tuple-element.28.new_values.values), custom_call_target="tpu_custom_call" | custom-call | tf_op jit(solution)/shard_map/mix/pallas_call | solution.py:358
  45.6 7.2 %all-to-all-start.1 = ((bf16[32,48,2,256]{3,2,1,0:T(2,128)(2,1)}), bf16[32,48,2,256]{3,2,1,0:T(2,128)(2,1)S(1)}, u32[]{:S(2)}, u32[]{:S(2)}) async-start(bf16[32,48,2,256]{3,2,1,0:T(2,128)(2,1)} %mix.1), calls=%async_computation.1 | async-start | bytes 3145728 | tf_op jit(solution)/shard_map/all_to_all | solution.py:516
  52.9 4.8 %split.1 = (bf16[1024,512]{1,0:T(8,128)(2,1)}, bf16[1024,512]{1,0:T(8,128)(2,1)}) custom-call(bf16[1024,2,512]{2,1,0:T(2,128)(2,1)} %bitcast.9), custom_call_target="tpu_custom_call" | custom-call | tf_op jit(solution)/shard_map/split/pallas_call | solution.py:297
  57.7 16.1 %attend.1 = (bf16[256,512]{1,0:T(8,128)(2,1)}, bf16[256,512]{1,0:T(8,128)(2,1)}, bf16[256,512]{1,0:T(8,128)(2,1)}, bf16[256,512]{1,0:T(8,128)(2,1)}, bf16[256,51...) custom-call(s32[32]{0:T(128)} %prior_len.1, ...), custom_call_target="tpu_custom_call" | custom-call | tf_op jit(solution)/shard_map/attend/pallas_call | solution.py:208
  73.8 3.1 %collective-permute-start.10 = (bf16[256,512]{1,0:T(8,128)(2,1)}, bf16[256,512]{1,0:T(8,128)(2,1)S(1)}, u32[]{:S(2)}, u32[]{:S(2)}) collective-permute-start(bf16[256,512]{1,0:T(8,128)(2,1)} %get-tuple-element.38), channel_id=1, source_target_pairs={{0,3},{1,0},{2,1},{3,2},{4,7},{5,4},{6,5},{7,6},{8,11},{9,8},{10,9... | collective-permute-start | bytes 786440 | tf_op jit(solution)/shard_map/ppermute | solution.py:24
  77.5 2.7 %collective-permute-start.6 = (bf16[256,512]{1,0:T(8,128)(2,1)}, bf16[256,512]{1,0:T(8,128)(2,1)S(1)}, u32[]{:S(2)}, u32[]{:S(2)}) collective-permute-start(bf16[256,512]{1,0:T(8,128)(2,1)} %get-tuple-element.32), channel_id=1, source_target_pairs={{0,3},{1,0},{2,1},{3,2},{4,7},{5,4},{6,5},{7,6},{8,11},{9,8},{10,9... | collective-permute-start | bytes 786440 | tf_op jit(solution)/shard_map/ppermute | solution.py:24
  80.2 3.7 %collective-permute-done.10 = bf16[256,512]{1,0:T(8,128)(2,1)S(1)} collective-permute-done((bf16[256,512]{1,0:T(8,128)(2,1)}, bf16[256,512]{1,0:T(8,128)(2,1)S(1)}, u32[]{:S(2)}, u32[]{:S(2)}) %collective-permute-start.10) | collective-permute-done | bytes 262176 | tf_op jit(solution)/shard_map/ppermute | solution.py:24
  85.6 3.6 %collective-permute-start.11 = (bf16[256,512]{1,0:T(8,128)(2,1)}, bf16[256,512]{1,0:T(8,128)(2,1)}, u32[]{:S(2)}, u32[]{:S(2)}) collective-permute-start(bf16[256,512]{1,0:T(8,128)(2,1)} %add_convert_fusion.5), channel_id=1, source_target_pairs={{0,3},{1,0},{2,1},{3,2},{4,7},{5,4},{6,5},{7,6},{8,11},{9,8},{10,9... | collective-permute-start | bytes 786440 | tf_op jit(solution)/shard_map/ppermute | solution.py:24
  90.5 4.5 %reorder.1 = bf16[32,80,2,256]{3,2,1,0:T(2,128)(2,1)} custom-call(s32[32]{0:T(128)} %slot_map.5, bf16[32,32,2,512]{3,2,1,0:T(2,128)(2,1)} %copy-done, bf16[32,48,2,256]{3,2,1,0:T(2,128)(2,1)} %copy-done.1), custom_call_target="tpu_custom_call" | custom-call | tf_op jit(solution)/shard_map/reorder/pallas_call | solution.py:407
  95.0 7.5 %all-to-all-start.2 = ((bf16[32,80,2,256]{3,2,1,0:T(2,128)(2,1)}), bf16[32,80,2,256]{3,2,1,0:T(2,128)(2,1)S(1)}, u32[]{:S(2)}, u32[]{:S(2)}) async-start(bf16[32,80,2,256]{3,2,1,0:T(2,128)(2,1)} %reorder.1), calls=%async_computation.2 | async-start | bytes 5242880 | tf_op jit(solution)/shard_map/all_to_all | solution.py:516
  103.7 6.3 %copy.20 = bf16[2048,2,768]{2,0,1:T(8,128)(2,1)} copy(bf16[2048,2,768]{2,1,0:T(2,128)(2,1)} %param.22) | data formatting | bytes 12582912 | tf_op args[8]
  110.0 3.3 %collective-permute-done.8 = bf16[256,512]{1,0:T(8,128)(2,1)S(1)} collective-permute-done((bf16[256,512]{1,0:T(8,128)(2,1)S(1)}, bf16[256,512]{1,0:T(8,128)(2,1)S(1)}, u32[]{:S(2)}, u32[]{:S(2)}) %collective-permute-start.8) | collective-permute-done | bytes 262176 | tf_op jit(solution)/shard_map/ppermute | solution.py:24
  114.8 3.2 %collective-permute-start.15 = (bf16[256,512]{1,0:T(8,128)(2,1)S(1)}, bf16[256,512]{1,0:T(8,128)(2,1)}, u32[]{:S(2)}, u32[]{:S(2)}) collective-permute-start(bf16[256,512]{1,0:T(8,128)(2,1)S(1)} %get-tuple-element.40.o1), channel_id=1, source_target_pairs={{0,3},{1,0},{2,1},{3,2},{4,7},{5,4},{6,5},{7,6},{8,11},{9,8},{10,9... | collective-permute-start | bytes 786440 | tf_op jit(solution)/shard_map/ppermute | solution.py:24
  118.0 3.2 %collective-permute-start.14 = (bf16[256,512]{1,0:T(8,128)(2,1)S(1)}, bf16[256,512]{1,0:T(8,128)(2,1)}, u32[]{:S(2)}, u32[]{:S(2)}) collective-permute-start(bf16[256,512]{1,0:T(8,128)(2,1)S(1)} %get-tuple-element.39.o0), channel_id=1, source_target_pairs={{0,3},{1,0},{2,1},{3,2},{4,7},{5,4},{6,5},{7,6},{8,11},{9,8},{10,9... | collective-permute-start | bytes 786440 | tf_op jit(solution)/shard_map/ppermute | solution.py:24
  121.3 3.9 %collective-permute-done.12.l0 = bf16[256,512]{1,0:T(8,128)(2,1)S(1)} collective-permute-done((bf16[256,512]{1,0:T(8,128)(2,1)S(1)}, bf16[256,512]{1,0:T(8,128)(2,1)S(1)}, u32[]{:S(2)}, u32[]{:S(2)}) %collective-permute-start.12) | collective-permute-done | bytes 262176 | tf_op jit(solution)/shard_map/ppermute | solution.py:24
  125.2 3.3 %collective-permute-start.17 = (bf16[256,512]{1,0:T(8,128)(2,1)}, bf16[256,512]{1,0:T(8,128)(2,1)}, u32[]{:S(2)}, u32[]{:S(2)}) collective-permute-start(bf16[256,512]{1,0:T(8,128)(2,1)} %collective-permute-done.15.r1), channel_id=1, source_target_pairs={{0,3},{1,0},{2,1},{3,2},{4,7},{5,4},{6,5},{7,6},{8,11},{9,8},{10,9... | collective-permute-start | bytes 786440 | tf_op jit(solution)/shard_map/ppermute | solution.py:24
  130.9 4.1 %collective-permute-done.16.f0 = bf16[256,512]{1,0:T(8,128)(2,1)} collective-permute-done((bf16[256,512]{1,0:T(8,128)(2,1)S(1)}, bf16[256,512]{1,0:T(8,128)(2,1)}, u32[]{:S(2)}, u32[]{:S(2)}) %collective-permute-start.16) | collective-permute-done | bytes 262176 | tf_op jit(solution)/shard_map/ppermute | solution.py:24
  135.0 11.0 %feed_forward.1 = (bf16[256,512]{1,0:T(8,128)(2,1)}, bf16[256,512]{1,0:T(8,128)(2,1)}, bf16[256,512]{1,0:T(8,128)(2,1)}, bf16[256,512]{1,0:T(8,128)(2,1)}, bf16[...) custom-call(bf16[256,512]{1,0:T(8,128)(2,1)} %copy-done.3, ...), custom_call_target="tpu_custom_call" | custom-call | tf_op jit(solution)/shard_map/feed_forward/pallas_call | solution.py:259
  146.1 3.0 %collective-permute-start.22 = (bf16[256,512]{1,0:T(8,128)(2,1)}, bf16[256,512]{1,0:T(8,128)(2,1)S(1)}, u32[]{:S(2)}, u32[]{:S(2)}) collective-permute-start(bf16[256,512]{1,0:T(8,128)(2,1)} %get-tuple-element.49), channel_id=1, source_target_pairs={{0,3},{1,0},{2,1},{3,2},{4,7},{5,4},{6,5},{7,6},{8,11},{9,8},{10,9... | collective-permute-start | bytes 786440 | tf_op jit(solution)/shard_map/ppermute | solution.py:24
  149.1 4.3 %collective-permute-done.22 = bf16[256,512]{1,0:T(8,128)(2,1)S(1)} collective-permute-done((bf16[256,512]{1,0:T(8,128)(2,1)}, bf16[256,512]{1,0:T(8,128)(2,1)S(1)}, u32[]{:S(2)}, u32[]{:S(2)}) %collective-permute-start.22) | collective-permute-done | bytes 262176 | tf_op jit(solution)/shard_map/ppermute | solution.py:24
  153.4 1.7 add_convert_fusion.1
  155.1 3.6 %collective-permute-start.23 = (bf16[256,512]{1,0:T(8,128)(2,1)}, bf16[256,512]{1,0:T(8,128)(2,1)}, u32[]{:S(2)}, u32[]{:S(2)}) collective-permute-start(bf16[256,512]{1,0:T(8,128)(2,1)} %add_convert_fusion.1), channel_id=1, source_target_pairs={{0,3},{1,0},{2,1},{3,2},{4,7},{5,4},{6,5},{7,6},{8,11},{9,8},{10,9... | collective-permute-start | bytes 786440 | tf_op jit(solution)/shard_map/ppermute | solution.py:24
  159.5 1.7 add_convert_fusion.3
  163.3 1.7 collective-permute-done.23
  172.6 5.1 %pages.1 = bf16[1,12,256,2,256]{4,3,2,1,0:T(2,128)(2,1)} custom-call(s32[32]{0:T(128)} %slot_map.5, s32[32]{0:T(128)} %prior_len.1, s32[192]{0:T(256)} %reshape.56.table, bf16[32,48,2,256]{3,2,1,0:T(2,128)(2,1)} %copy-done.1, bf16[32,80,2,256]{3,2,1,0:T(2,128)(2,1)} %copy-done.2), custom_call_target="tpu_custom_call" | custom-call | tf_op jit(solution)/shard_map/pages/pallas_call | solution.py:484
  (100 shorter events, 26.9 us)
Async XLA Ops:
  0.7 22.2 %copy-start.19 = (f32[2048]{0:T(1024)S(1)}, f32[2048]{0:T(1024)}, u32[]{:S(2)}) copy-start(f32[2048]{0:T(1024)} %param.15) | copy-start | bytes 24580
  0.7 22.8 %copy-start.20 = (f32[2048]{0:T(1024)S(1)}, f32[2048]{0:T(1024)}, u32[]{:S(2)}) copy-start(f32[2048]{0:T(1024)} %param.16) | copy-start | bytes 24580
  0.7 38.6 %all-to-all-start = ((bf16[32,32,2,512]{3,2,1,0:T(2,128)(2,1)}), bf16[32,32,2,512]{3,2,1,0:T(2,128)(2,1)S(1)}, u32[]{:S(2)}, u32[]{:S(2)}) async-start(bf16[32,32,2,512]{3,2,1,0:T(2,128)(2,1)} %bitcast.8), calls=%async_computation | async-start | bytes 4194304 | tf_op jit(solution)/shard_map/all_to_all | solution.py:516
  9.2 10.5 %collective-permute-start = (bf16[256,512]{1,0:T(8,128)(2,1)S(1)}, bf16[256,512]{1,0:T(8,128)(2,1)S(1)}, u32[]{:S(2)}, u32[]{:S(2)}) collective-permute-start(bf16[256,512]{1,0:T(8,128)(2,1)S(1)} %get-tuple-element.53.o0), channel_id=1, source_target_pairs={{0,1},{1,2},{2,3},{3,0},{4,5},{5,6},{6,7},{7,4},{8,9},{9,10},{10,1... | collective-permute-start | bytes 786440 | tf_op jit(solution)/shard_map/ppermute | solution.py:24
  10.8 9.2 %collective-permute-start.3 = (bf16[256,512]{1,0:T(8,128)(2,1)S(1)}, bf16[256,512]{1,0:T(8,128)(2,1)S(1)}, u32[]{:S(2)}, u32[]{:S(2)}) collective-permute-start(bf16[256,512]{1,0:T(8,128)(2,1)S(1)} %get-tuple-element.52.o1), channel_id=1, source_target_pairs={{0,3},{1,0},{2,1},{3,2},{4,7},{5,4},{6,5},{7,6},{8,11},{9,8},{10,9... | collective-permute-start | bytes 786440 | tf_op jit(solution)/shard_map/ppermute | solution.py:24
  12.5 13.5 %collective-permute-start.1 = (bf16[256,512]{1,0:T(8,128)(2,1)S(1)}, bf16[256,512]{1,0:T(8,128)(2,1)S(1)}, u32[]{:S(2)}, u32[]{:S(2)}) collective-permute-start(bf16[256,512]{1,0:T(8,128)(2,1)S(1)} %get-tuple-element.52.o1), channel_id=1, source_target_pairs={{0,1},{1,2},{2,3},{3,0},{4,5},{5,6},{6,7},{7,4},{8,9},{9,10},{10,1... | collective-permute-start | bytes 786440 | tf_op jit(solution)/shard_map/ppermute | solution.py:24
  12.8 13.1 %collective-permute-start.2 = (bf16[256,512]{1,0:T(8,128)(2,1)S(1)}, bf16[256,512]{1,0:T(8,128)(2,1)}, u32[]{:S(2)}, u32[]{:S(2)}) collective-permute-start(bf16[256,512]{1,0:T(8,128)(2,1)S(1)} %get-tuple-element.53.o0), channel_id=1, source_target_pairs={{0,3},{1,0},{2,1},{3,2},{4,7},{5,4},{6,5},{7,6},{8,11},{9,8},{10,9... | collective-permute-start | bytes 786440 | tf_op jit(solution)/shard_map/ppermute | solution.py:24
  19.6 10.7 %collective-permute-start.4 = (bf16[256,512]{1,0:T(8,128)(2,1)S(1)}, bf16[256,512]{1,0:T(8,128)(2,1)}, u32[]{:S(2)}, u32[]{:S(2)}) collective-permute-start(bf16[256,512]{1,0:T(8,128)(2,1)S(1)} %collective-permute-done.l0), channel_id=1, source_target_pairs={{0,1},{1,2},{2,3},{3,0},{4,5},{5,6},{6,7},{7,4},{8,9},{9,10},{10,1... | collective-permute-start | bytes 786440 | tf_op jit(solution)/shard_map/ppermute | solution.py:24
  20.0 10.4 %collective-permute-start.5 = (bf16[256,512]{1,0:T(8,128)(2,1)S(1)}, bf16[256,512]{1,0:T(8,128)(2,1)}, u32[]{:S(2)}, u32[]{:S(2)}) collective-permute-start(bf16[256,512]{1,0:T(8,128)(2,1)S(1)} %collective-permute-done.3.r1), channel_id=1, source_target_pairs={{0,3},{1,0},{2,1},{3,2},{4,7},{5,4},{6,5},{7,6},{8,11},{9,8},{10,9... | collective-permute-start | bytes 786440 | tf_op jit(solution)/shard_map/ppermute | solution.py:24
  45.6 43.6 %all-to-all-start.1 = ((bf16[32,48,2,256]{3,2,1,0:T(2,128)(2,1)}), bf16[32,48,2,256]{3,2,1,0:T(2,128)(2,1)S(1)}, u32[]{:S(2)}, u32[]{:S(2)}) async-start(bf16[32,48,2,256]{3,2,1,0:T(2,128)(2,1)} %mix.1), calls=%async_computation.1 | async-start | bytes 3145728 | tf_op jit(solution)/shard_map/all_to_all | solution.py:516
  73.8 10.1 %collective-permute-start.10 = (bf16[256,512]{1,0:T(8,128)(2,1)}, bf16[256,512]{1,0:T(8,128)(2,1)S(1)}, u32[]{:S(2)}, u32[]{:S(2)}) collective-permute-start(bf16[256,512]{1,0:T(8,128)(2,1)} %get-tuple-element.38), channel_id=1, source_target_pairs={{0,3},{1,0},{2,1},{3,2},{4,7},{5,4},{6,5},{7,6},{8,11},{9,8},{10,9... | collective-permute-start | bytes 786440 | tf_op jit(solution)/shard_map/ppermute | solution.py:24
  76.9 25.6 %collective-permute-start.7 = (bf16[256,512]{1,0:T(8,128)(2,1)}, bf16[256,512]{1,0:T(8,128)(2,1)}, u32[]{:S(2)}, u32[]{:S(2)}) collective-permute-start(bf16[256,512]{1,0:T(8,128)(2,1)} %get-tuple-element.34), channel_id=1, source_target_pairs={{0,1},{1,2},{2,3},{3,0},{4,5},{5,6},{6,7},{7,4},{8,9},{9,10},{10,1... | collective-permute-start | bytes 786440 | tf_op jit(solution)/shard_map/ppermute | solution.py:24
  76.9 33.1 %collective-permute-start.9 = (bf16[256,512]{1,0:T(8,128)(2,1)}, bf16[256,512]{1,0:T(8,128)(2,1)S(1)}, u32[]{:S(2)}, u32[]{:S(2)}) collective-permute-start(bf16[256,512]{1,0:T(8,128)(2,1)} %get-tuple-element.36), channel_id=1, source_target_pairs={{0,1},{1,2},{2,3},{3,0},{4,5},{5,6},{6,7},{7,4},{8,9},{9,10},{10,1... | collective-permute-start | bytes 786440 | tf_op jit(solution)/shard_map/ppermute | solution.py:24
  77.5 32.5 %collective-permute-start.6 = (bf16[256,512]{1,0:T(8,128)(2,1)}, bf16[256,512]{1,0:T(8,128)(2,1)S(1)}, u32[]{:S(2)}, u32[]{:S(2)}) collective-permute-start(bf16[256,512]{1,0:T(8,128)(2,1)} %get-tuple-element.32), channel_id=1, source_target_pairs={{0,3},{1,0},{2,1},{3,2},{4,7},{5,4},{6,5},{7,6},{8,11},{9,8},{10,9... | collective-permute-start | bytes 786440 | tf_op jit(solution)/shard_map/ppermute | solution.py:24
  85.6 24.4 %collective-permute-start.11 = (bf16[256,512]{1,0:T(8,128)(2,1)}, bf16[256,512]{1,0:T(8,128)(2,1)}, u32[]{:S(2)}, u32[]{:S(2)}) collective-permute-start(bf16[256,512]{1,0:T(8,128)(2,1)} %add_convert_fusion.5), channel_id=1, source_target_pairs={{0,3},{1,0},{2,1},{3,2},{4,7},{5,4},{6,5},{7,6},{8,11},{9,8},{10,9... | collective-permute-start | bytes 786440 | tf_op jit(solution)/shard_map/ppermute | solution.py:24
  95.0 76.2 %all-to-all-start.2 = ((bf16[32,80,2,256]{3,2,1,0:T(2,128)(2,1)}), bf16[32,80,2,256]{3,2,1,0:T(2,128)(2,1)S(1)}, u32[]{:S(2)}, u32[]{:S(2)}) async-start(bf16[32,80,2,256]{3,2,1,0:T(2,128)(2,1)} %reorder.1), calls=%async_computation.2 | async-start | bytes 5242880 | tf_op jit(solution)/shard_map/all_to_all | solution.py:516
  103.6 9.8 %collective-permute-start.8 = (bf16[256,512]{1,0:T(8,128)(2,1)S(1)}, bf16[256,512]{1,0:T(8,128)(2,1)S(1)}, u32[]{:S(2)}, u32[]{:S(2)}) collective-permute-start(bf16[256,512]{1,0:T(8,128)(2,1)S(1)} %add_convert_fusion.7), channel_id=1, source_target_pairs={{0,1},{1,2},{2,3},{3,0},{4,5},{5,6},{6,7},{7,4},{8,9},{9,10},{10,1... | collective-permute-start | bytes 786440 | tf_op jit(solution)/shard_map/ppermute | solution.py:24
  114.7 10.5 %collective-permute-start.12 = (bf16[256,512]{1,0:T(8,128)(2,1)S(1)}, bf16[256,512]{1,0:T(8,128)(2,1)S(1)}, u32[]{:S(2)}, u32[]{:S(2)}) collective-permute-start(bf16[256,512]{1,0:T(8,128)(2,1)S(1)} %get-tuple-element.39.o0), channel_id=1, source_target_pairs={{0,1},{1,2},{2,3},{3,0},{4,5},{5,6},{6,7},{7,4},{8,9},{9,10},{10,1... | collective-permute-start | bytes 786440 | tf_op jit(solution)/shard_map/ppermute | solution.py:24
  114.8 10.4 %collective-permute-start.15 = (bf16[256,512]{1,0:T(8,128)(2,1)S(1)}, bf16[256,512]{1,0:T(8,128)(2,1)}, u32[]{:S(2)}, u32[]{:S(2)}) collective-permute-start(bf16[256,512]{1,0:T(8,128)(2,1)S(1)} %get-tuple-element.40.o1), channel_id=1, source_target_pairs={{0,3},{1,0},{2,1},{3,2},{4,7},{5,4},{6,5},{7,6},{8,11},{9,8},{10,9... | collective-permute-start | bytes 786440 | tf_op jit(solution)/shard_map/ppermute | solution.py:24
  118.0 12.9 %collective-permute-start.13 = (bf16[256,512]{1,0:T(8,128)(2,1)S(1)}, bf16[256,512]{1,0:T(8,128)(2,1)}, u32[]{:S(2)}, u32[]{:S(2)}) collective-permute-start(bf16[256,512]{1,0:T(8,128)(2,1)S(1)} %get-tuple-element.40.o1), channel_id=1, source_target_pairs={{0,1},{1,2},{2,3},{3,0},{4,5},{5,6},{6,7},{7,4},{8,9},{9,10},{10,1... | collective-permute-start | bytes 786440 | tf_op jit(solution)/shard_map/ppermute | solution.py:24
  118.0 12.9 %collective-permute-start.14 = (bf16[256,512]{1,0:T(8,128)(2,1)S(1)}, bf16[256,512]{1,0:T(8,128)(2,1)}, u32[]{:S(2)}, u32[]{:S(2)}) collective-permute-start(bf16[256,512]{1,0:T(8,128)(2,1)S(1)} %get-tuple-element.39.o0), channel_id=1, source_target_pairs={{0,3},{1,0},{2,1},{3,2},{4,7},{5,4},{6,5},{7,6},{8,11},{9,8},{10,9... | collective-permute-start | bytes 786440 | tf_op jit(solution)/shard_map/ppermute | solution.py:24
  125.2 9.8 %collective-permute-start.16 = (bf16[256,512]{1,0:T(8,128)(2,1)S(1)}, bf16[256,512]{1,0:T(8,128)(2,1)}, u32[]{:S(2)}, u32[]{:S(2)}) collective-permute-start(bf16[256,512]{1,0:T(8,128)(2,1)S(1)} %collective-permute-done.12.l0), channel_id=1, source_target_pairs={{0,1},{1,2},{2,3},{3,0},{4,5},{5,6},{6,7},{7,4},{8,9},{9,10},{10,1... | collective-permute-start | bytes 786440 | tf_op jit(solution)/shard_map/ppermute | solution.py:24
  125.2 9.8 %collective-permute-start.17 = (bf16[256,512]{1,0:T(8,128)(2,1)}, bf16[256,512]{1,0:T(8,128)(2,1)}, u32[]{:S(2)}, u32[]{:S(2)}) collective-permute-start(bf16[256,512]{1,0:T(8,128)(2,1)} %collective-permute-done.15.r1), channel_id=1, source_target_pairs={{0,3},{1,0},{2,1},{3,2},{4,7},{5,4},{6,5},{7,6},{8,11},{9,8},{10,9... | collective-permute-start | bytes 786440 | tf_op jit(solution)/shard_map/ppermute | solution.py:24
  129.7 32.8 %copy-start.23 = (s32[32,6]{0,1:T(8,128)S(1)}, s32[32,6]{0,1:T(8,128)}, u32[]{:S(2)}) copy-start(s32[32,6]{0,1:T(8,128)} %param.27) | copy-start | bytes 2308
  146.0 23.1 %copy-start.4 = (bf16[256,512]{1,0:T(8,128)(2,1)S(1)}, bf16[256,512]{1,0:T(8,128)(2,1)}, u32[]{:S(2)}) copy-start(bf16[256,512]{1,0:T(8,128)(2,1)} %copy-done.3) | copy-start | bytes 786436
  146.1 23.1 %copy-start.12 = (bf16[256,512]{1,0:T(8,128)(2,1)S(1)}, bf16[256,512]{1,0:T(8,128)(2,1)}, u32[]{:S(2)}) copy-start(bf16[256,512]{1,0:T(8,128)(2,1)} %get-tuple-element.42) | copy-start | bytes 786436
  146.1 7.3 %collective-permute-start.22 = (bf16[256,512]{1,0:T(8,128)(2,1)}, bf16[256,512]{1,0:T(8,128)(2,1)S(1)}, u32[]{:S(2)}, u32[]{:S(2)}) collective-permute-start(bf16[256,512]{1,0:T(8,128)(2,1)} %get-tuple-element.49), channel_id=1, source_target_pairs={{0,3},{1,0},{2,1},{3,2},{4,7},{5,4},{6,5},{7,6},{8,11},{9,8},{10,9... | collective-permute-start | bytes 786440 | tf_op jit(solution)/shard_map/ppermute | solution.py:24
  149.1 10.4 %collective-permute-start.19 = (bf16[256,512]{1,0:T(8,128)(2,1)}, bf16[256,512]{1,0:T(8,128)(2,1)S(1)}, u32[]{:S(2)}, u32[]{:S(2)}) collective-permute-start(bf16[256,512]{1,0:T(8,128)(2,1)} %get-tuple-element.45), channel_id=1, source_target_pairs={{0,1},{1,2},{2,3},{3,0},{4,5},{5,6},{6,7},{7,4},{8,9},{9,10},{10,1... | collective-permute-start | bytes 786440 | tf_op jit(solution)/shard_map/ppermute | solution.py:24
  149.1 14.2 %collective-permute-start.21 = (bf16[256,512]{1,0:T(8,128)(2,1)}, bf16[256,512]{1,0:T(8,128)(2,1)S(1)}, u32[]{:S(2)}, u32[]{:S(2)}) collective-permute-start(bf16[256,512]{1,0:T(8,128)(2,1)} %get-tuple-element.47), channel_id=1, source_target_pairs={{0,1},{1,2},{2,3},{3,0},{4,5},{5,6},{6,7},{7,4},{8,9},{9,10},{10,1... | collective-permute-start | bytes 786440 | tf_op jit(solution)/shard_map/ppermute | solution.py:24
  155.1 9.9 %collective-permute-start.23 = (bf16[256,512]{1,0:T(8,128)(2,1)}, bf16[256,512]{1,0:T(8,128)(2,1)}, u32[]{:S(2)}, u32[]{:S(2)}) collective-permute-start(bf16[256,512]{1,0:T(8,128)(2,1)} %add_convert_fusion.1), channel_id=1, source_target_pairs={{0,3},{1,0},{2,1},{3,2},{4,7},{5,4},{6,5},{7,6},{8,11},{9,8},{10,9... | collective-permute-start | bytes 786440 | tf_op jit(solution)/shard_map/ppermute | solution.py:24
  158.7 9.1 %collective-permute-start.18 = (bf16[256,512]{1,0:T(8,128)(2,1)}, bf16[256,512]{1,0:T(8,128)(2,1)}, u32[]{:S(2)}, u32[]{:S(2)}) collective-permute-start(bf16[256,512]{1,0:T(8,128)(2,1)} %get-tuple-element.43), channel_id=1, source_target_pairs={{0,3},{1,0},{2,1},{3,2},{4,7},{5,4},{6,5},{7,6},{8,11},{9,8},{10,9... | collective-permute-start | bytes 786440 | tf_op jit(solution)/shard_map/ppermute | solution.py:24
  161.3 7.9 %collective-permute-start.20 = (bf16[256,512]{1,0:T(8,128)(2,1)}, bf16[256,512]{1,0:T(8,128)(2,1)}, u32[]{:S(2)}, u32[]{:S(2)}) collective-permute-start(bf16[256,512]{1,0:T(8,128)(2,1)} %add_convert_fusion.3), channel_id=1, source_target_pairs={{0,1},{1,2},{2,3},{3,0},{4,5},{5,6},{6,7},{7,4},{8,9},{9,10},{10,1... | collective-permute-start | bytes 786440 | tf_op jit(solution)/shard_map/ppermute | solution.py:24
  (20 other events, 223.8 us)

commit v3 on v2

--- a/solution.py
+++ b/solution.py
@@ -1,3 +1,5 @@
+import functools
+
 import jax
 import jax.numpy as jnp
 from jax import lax
@@ -68,7 +70,7 @@
                 normed[pl.ds(part * half + at, step), slot * width : (slot + 1) * width] = value.astype(BF)
             return carry
 
-        lax.fori_loop(0, half // step, body, 0)
+        lax.fori_loop(0, half // step, body, 0, unroll=2)
 
 
 def project_kernel(
@@ -166,34 +168,35 @@
             lanes = pl.ds(pl.multiple_of(pair * 128, 128), 128)
             query = queries[rows, lanes]
             old_key, new_key = old_keys[:, lanes], new_keys[:seen, lanes]
-            old_value, new_value = old_values[:, lanes], new_values[:seen, lanes]
+            ones = jnp.ones((cached, 128), BF)
+            old_value = jnp.concatenate([old_values[:, lanes], ones], axis=1)
+            new_value = jnp.concatenate([new_values[:seen, lanes], ones[:seen]], axis=1)
             lane = lax.broadcasted_iota(jnp.int32, (step, 128), 1)
             old_allowed = lax.broadcasted_iota(jnp.int32, (1, cached), 1) < prior
-            new_allowed = lax.broadcasted_iota(jnp.int32, (step, seen), 1) <= lax.broadcasted_iota(
-                jnp.int32, (step, seen), 0
-            ) + part * step
+            allowed = lax.broadcasted_iota(jnp.int32, (step, step), 1) <= lax.broadcasted_iota(jnp.int32, (step, step), 0)
             results = []
             for head in range(2):
                 own = (lane < HEAD_DIM) if head == 0 else (lane >= HEAD_DIM)
                 masked = jnp.where(own, query, jnp.zeros((), BF))
                 old_score = lax.dot_general(masked, old_key, contract, preferred_element_type=F32)
-                old_score = jnp.where(old_allowed, old_score, MASK_FILL)
                 new_score = lax.dot_general(masked, new_key, contract, preferred_element_type=F32)
-                new_score = jnp.where(new_allowed, new_score, MASK_FILL)
-                highest = jnp.maximum(
-                    jnp.max(old_score, axis=1, keepdims=True), jnp.max(new_score, axis=1, keepdims=True)
+                scores = [jnp.where(old_allowed, old_score, MASK_FILL)]
+                rows_of = [old_value]
+                if part:
+                    scores.append(new_score[:, : part * step])
+                    rows_of.append(new_value[: part * step])
+                scores.append(jnp.where(allowed, new_score[:, part * step :], MASK_FILL))
+                rows_of.append(new_value[part * step :])
+                highest = functools.reduce(jnp.maximum, [jnp.max(score, axis=1, keepdims=True) for score in scores])
+                value = sum(
+                    jnp.dot(jnp.exp(score - highest).astype(BF), these, preferred_element_type=F32)
+                    for score, these in zip(scores, rows_of)
                 )
-                old_weight = jnp.exp(old_score - highest)
-                new_weight = jnp.exp(new_score - highest)
-                total = jnp.sum(old_weight, axis=1, keepdims=True) + jnp.sum(new_weight, axis=1, keepdims=True)
-                value = jnp.dot(old_weight.astype(BF), old_value, preferred_element_type=F32) + jnp.dot(
-                    new_weight.astype(BF), new_value, preferred_element_type=F32
-                )
-                results.append(value / total)
+                results.append(value[:, :128] / value[:, 128:])
             mixed[rows, lanes] = jnp.where(lane < HEAD_DIM, results[0], results[1]).astype(BF)
             return carry
 
-        lax.fori_loop(0, width // 128, body, 0)
+        lax.fori_loop(0, width // 128, body, 0, unroll=4)
     for copy in copies:
         copy.wait()
     for part in range(rows_all // step):
@@ -367,7 +370,7 @@
         ],
         compiler_params=PARAMS,
         name="mix",
-    )(slot_map, pieces, keys, values)
+    )(slot_map, pltpu.with_memory_space_constraint(pieces, VMEM), keys, values)
 
 
 def reorder_kernel(slot_map, pieces, mixed, out, owners, stage, sems):
@@ -407,7 +410,7 @@
     return pl.pallas_call(
         reorder_kernel,
         out_shape=jax.ShapeDtypeStruct((count, 2 * late + 2 * fresh, 2, width // 2), BF),
-        in_specs=specs("s", "v", "a"),
+        in_specs=specs("s", "v", "v"),
         out_specs=specs("a")[0],
         scratch_shapes=[
             pltpu.SMEM((count,), jnp.int32),
@@ -416,7 +419,7 @@
         ],
         compiler_params=PARAMS,
         name="reorder",
-    )(slot_map, pieces, mixed)
+    )(slot_map, pltpu.with_memory_space_constraint(pieces, VMEM), pltpu.with_memory_space_constraint(mixed, VMEM))
 
 
 def pages_kernel(slot_map, prior_len, table, mixed, rest, out, owners, full, blank, sems):
@@ -484,7 +487,7 @@
     return pl.pallas_call(
         pages_kernel,
         out_shape=jax.ShapeDtypeStruct((1, 2 * (cached + fresh) // BLOCK, BLOCK, 2, width), BF),
-        in_specs=specs("s", "s", "s", "a", "a"),
+        in_specs=specs("s", "s", "s", "a", "v"),
         out_specs=specs("a")[0],
         scratch_shapes=[
             pltpu.SMEM((count,), jnp.int32),
@@ -494,7 +497,7 @@
         ],
         compiler_params=PARAMS,
         name="pages",
-    )(slot_map, prior_len, table, mixed, rest)
+    )(slot_map, prior_len, table, mixed, pltpu.with_memory_space_constraint(rest, VMEM))
 
 
 def rotary_tables(prior_count, rows):

time: 179 us -> 173 us (0.966)
  local copies, waits for them, and re-layouts: 14.3 us -> 10.2 us
  Pallas kernels: 55.5 us -> 53.2 us
    pallas_call x1, Pallas kernels: 16.1 us -> 11.8 us  [attend(): pl.pallas_call(attend_kernel, out_shape=(jax.ShapeDtypeStruct((rows // 2,...]
    unnamed x52 -> x46, local copies, waits for them, and re-layouts: 10.6 us -> 6.45 us
    pallas_call x1, Pallas kernels: 5.1 us -> 7.39 us  [pages(): pl.pallas_call(pages_kernel, out_shape=jax.ShapeDtypeStruct((1, 2 * (cach...]
  transfers between devices with their start and end apart: 27 -> 27, of which waited for: 12 -> 12; matrix products, arithmetic and copies ran while one was open for 13% -> 14% of each run, Pallas kernels for 25% -> 24%
where the time goes in v3:
time: 173 us; the launch traced here: 172 us
  starting transfers between devices  61 us (35%)
  Pallas kernels  53.2 us (31%)
  waiting for transfers between devices  33.1 us (19%)
  other arithmetic  13.2 us (8%)
  local copies, waits for them, and re-layouts  10.2 us (6%)
    ppermute x24, starting transfers between devices, shift_by(): return lax.ppermute(value, 'tp', [(i, (i + step) % 4) for i in range(4)])  37.7 us
    ppermute x24, waiting for transfers between devices, shift_by(): return lax.ppermute(value, 'tp', [(i, (i + step) % 4) for i in range(4)])  33.1 us
    all_to_all x3, starting transfers between devices, exchange(): lax.all_to_all(pieces, 'req', split_axis=0, concat_axis=0, tiled=True)  23.2 us
    pallas_call x1, Pallas kernels, attend(): pl.pallas_call(attend_kernel, out_shape=(jax.ShapeDtypeStruct((rows // 2,...  11.8 us
    pallas_call x1, Pallas kernels, feed_forward(): pl.pallas_call(forward_kernel, out_shape=(jax.ShapeDtypeStruct((half, wid...  11 us
    pallas_call x1, Pallas kernels, project(): pl.pallas_call(project_kernel, out_shape=(out, out, out), in_specs=specs(...  8.85 us
    pallas_call x1, Pallas kernels, pages(): pl.pallas_call(pages_kernel, out_shape=jax.ShapeDtypeStruct((1, 2 * (cach...  7.39 us
    unnamed x46, local copies, waits for them, and re-layouts  6.45 us
  transfers between devices with their start and end apart: 27, of which 12 were waited for; matrix products, arithmetic and copies ran while one was open for 14% of the time, Pallas kernels for 24%

profile of v3, /device:TPU:0, one launch (start us, length us, event | category | flops | bytes accessed | tf_op | source)
XLA Modules:
  0.0 171.9 jit_solution(7044762649197566455)
XLA Ops:
  0.7 8.4 %all-to-all-start = ((bf16[32,32,2,512]{3,2,1,0:T(2,128)(2,1)}), bf16[32,32,2,512]{3,2,1,0:T(2,128)(2,1)S(1)}, u32[]{:S(2)}, u32[]{:S(2)}) async-start(bf16[32,32,2,512]{3,2,1,0:T(2,128)(2,1)} %bitcast.8), calls=%async_computation | async-start | bytes 4194304 | tf_op jit(solution)/shard_map/all_to_all | solution.py:519
  12.8 2.9 %collective-permute-start.2 = (bf16[256,512]{1,0:T(8,128)(2,1)S(1)}, bf16[256,512]{1,0:T(8,128)(2,1)}, u32[]{:S(2)}, u32[]{:S(2)}) collective-permute-start(bf16[256,512]{1,0:T(8,128)(2,1)S(1)} %get-tuple-element.53.o0), channel_id=1, source_target_pairs={{0,3},{1,0},{2,1},{3,2},{4,7},{5,4},{6,5},{7,6},{8,11},{9,8},{10,9... | collective-permute-start | bytes 786440 | tf_op jit(solution)/shard_map/ppermute | solution.py:26
  17.0 2.7 %collective-permute-done.l0 = bf16[256,512]{1,0:T(8,128)(2,1)S(1)} collective-permute-done((bf16[256,512]{1,0:T(8,128)(2,1)S(1)}, bf16[256,512]{1,0:T(8,128)(2,1)S(1)}, u32[]{:S(2)}, u32[]{:S(2)}) %collective-permute-start) | collective-permute-done | bytes 262176 | tf_op jit(solution)/shard_map/ppermute | solution.py:26
  20.0 2.9 %collective-permute-start.5 = (bf16[256,512]{1,0:T(8,128)(2,1)S(1)}, bf16[256,512]{1,0:T(8,128)(2,1)}, u32[]{:S(2)}, u32[]{:S(2)}) collective-permute-start(bf16[256,512]{1,0:T(8,128)(2,1)S(1)} %collective-permute-done.3.r1), channel_id=1, source_target_pairs={{0,3},{1,0},{2,1},{3,2},{4,7},{5,4},{6,5},{7,6},{8,11},{9,8},{10,9... | collective-permute-start | bytes 786440 | tf_op jit(solution)/shard_map/ppermute | solution.py:26
  24.1 1.9 %fusion = (f32[512,128]{1,0:T(8,128)}, f32[512,128]{1,0:T(8,128)}, f32[512,128]{1,0:T(8,128)}) fusion(f32[128]{0:T(128)S(1)} %compare_select_fusion.2, f32[512]{0:T(512)S(1)} %add_convert_fusion.8, pred[128]{0:T(512)(128)(4,1)S(1)} %get-tuple-element.57, pred[128]{0:T(512)(128)(4,1)S(1)} %get-tuple-element.58), kind=kLoop, calls=%fused_computation.12 | loop fusion | flops 262144 | bytes 789248 | tf_op jit(solution)/shard_map/jit(_where)/select_n | solution.py:514
  26.0 4.4 %collective-permute-done.4.f0 = bf16[256,512]{1,0:T(8,128)(2,1)} collective-permute-done((bf16[256,512]{1,0:T(8,128)(2,1)S(1)}, bf16[256,512]{1,0:T(8,128)(2,1)}, u32[]{:S(2)}, u32[]{:S(2)}) %collective-permute-start.4) | collective-permute-done | bytes 262176 | tf_op jit(solution)/shard_map/ppermute | solution.py:26
  30.4 8.8 %project.1 = (bf16[512,512]{1,0:T(8,128)(2,1)}, bf16[512,512]{1,0:T(8,128)(2,1)}, bf16[512,512]{1,0:T(8,128)(2,1)}) custom-call(bf16[256,512]{1,0:T(8,128)(2,1)} %copy-done.6, bf16[256,512]{1,0:T(8,128)(2,1)} %copy-done.5, bf16[256,512]{1,0:T(8,128)(2,1)} %copy-done.13, bf16[256,512]{1,0:T(8,128)(2,1)} %copy-done.15, ...), custom_call_target="tpu_custom_call" | custom-call | tf_op jit(solution)/shard_map/project/pallas_call | solution.py:131
  39.3 4.4 %mix.1 = bf16[32,48,2,256]{3,2,1,0:T(2,128)(2,1)} custom-call(s32[32]{0:T(128)} %slot_map.5, bf16[32,32,2,512]{3,2,1,0:T(2,128)(2,1)S(1)} %all-to-all-done.pieces, bf16[512,512]{1,0:T(8,128)(2,1)} %get-tuple-element.27.new_keys.keys, bf16[512,512]{1,0:T(8,128)(2,1)} %get-tuple-element.28.new_values.values), custom_call_target="tpu_custom_call" | custom-call | tf_op jit(solution)/shard_map/mix/pallas_call | solution.py:361
  43.6 7.5 %all-to-all-start.1 = ((bf16[32,48,2,256]{3,2,1,0:T(2,128)(2,1)}), bf16[32,48,2,256]{3,2,1,0:T(2,128)(2,1)}, u32[]{:S(2)}, u32[]{:S(2)}) async-start(bf16[32,48,2,256]{3,2,1,0:T(2,128)(2,1)} %mix.1), calls=%async_computation.1 | async-start | bytes 3145728 | tf_op jit(solution)/shard_map/all_to_all | solution.py:519
  51.2 4.8 %split.1 = (bf16[1024,512]{1,0:T(8,128)(2,1)}, bf16[1024,512]{1,0:T(8,128)(2,1)}) custom-call(bf16[1024,2,512]{2,1,0:T(2,128)(2,1)} %bitcast.9), custom_call_target="tpu_custom_call" | custom-call | tf_op jit(solution)/shard_map/split/pallas_call | solution.py:300
  56.0 11.8 %attend.1 = (bf16[256,512]{1,0:T(8,128)(2,1)}, bf16[256,512]{1,0:T(8,128)(2,1)}, bf16[256,512]{1,0:T(8,128)(2,1)}, bf16[256,512]{1,0:T(8,128)(2,1)}, bf16[256,51...) custom-call(s32[32]{0:T(128)} %prior_len.1, ...), custom_call_target="tpu_custom_call" | custom-call | tf_op jit(solution)/shard_map/attend/pallas_call | solution.py:211
  67.8 3.1 %collective-permute-start.10 = (bf16[256,512]{1,0:T(8,128)(2,1)}, bf16[256,512]{1,0:T(8,128)(2,1)S(1)}, u32[]{:S(2)}, u32[]{:S(2)}) collective-permute-start(bf16[256,512]{1,0:T(8,128)(2,1)} %get-tuple-element.38), channel_id=1, source_target_pairs={{0,3},{1,0},{2,1},{3,2},{4,7},{5,4},{6,5},{7,6},{8,11},{9,8},{10,9... | collective-permute-start | bytes 786440 | tf_op jit(solution)/shard_map/ppermute | solution.py:26
  71.4 2.7 %collective-permute-start.6 = (bf16[256,512]{1,0:T(8,128)(2,1)}, bf16[256,512]{1,0:T(8,128)(2,1)S(1)}, u32[]{:S(2)}, u32[]{:S(2)}) collective-permute-start(bf16[256,512]{1,0:T(8,128)(2,1)} %get-tuple-element.32), channel_id=1, source_target_pairs={{0,3},{1,0},{2,1},{3,2},{4,7},{5,4},{6,5},{7,6},{8,11},{9,8},{10,9... | collective-permute-start | bytes 786440 | tf_op jit(solution)/shard_map/ppermute | solution.py:26
  74.1 3.7 %collective-permute-done.10 = bf16[256,512]{1,0:T(8,128)(2,1)S(1)} collective-permute-done((bf16[256,512]{1,0:T(8,128)(2,1)}, bf16[256,512]{1,0:T(8,128)(2,1)S(1)}, u32[]{:S(2)}, u32[]{:S(2)}) %collective-permute-start.10) | collective-permute-done | bytes 262176 | tf_op jit(solution)/shard_map/ppermute | solution.py:26
  77.9 1.7 add_convert_fusion.5
  79.6 3.6 %collective-permute-start.11 = (bf16[256,512]{1,0:T(8,128)(2,1)}, bf16[256,512]{1,0:T(8,128)(2,1)}, u32[]{:S(2)}, u32[]{:S(2)}) collective-permute-start(bf16[256,512]{1,0:T(8,128)(2,1)} %add_convert_fusion.5), channel_id=1, source_target_pairs={{0,3},{1,0},{2,1},{3,2},{4,7},{5,4},{6,5},{7,6},{8,11},{9,8},{10,9... | collective-permute-start | bytes 786440 | tf_op jit(solution)/shard_map/ppermute | solution.py:26
  83.2 5.0 %reorder.1 = bf16[32,80,2,256]{3,2,1,0:T(2,128)(2,1)} custom-call(s32[32]{0:T(128)} %slot_map.5, bf16[32,32,2,512]{3,2,1,0:T(2,128)(2,1)S(1)} %all-to-all-done.pieces, bf16[32,48,2,256]{3,2,1,0:T(2,128)(2,1)} %all-to-all-done.1.mixed), custom_call_target="tpu_custom_call" | custom-call | tf_op jit(solution)/shard_map/reorder/pallas_call | solution.py:410
  88.1 7.3 %all-to-all-start.2 = ((bf16[32,80,2,256]{3,2,1,0:T(2,128)(2,1)}), bf16[32,80,2,256]{3,2,1,0:T(2,128)(2,1)S(1)}, u32[]{:S(2)}, u32[]{:S(2)}) async-start(bf16[32,80,2,256]{3,2,1,0:T(2,128)(2,1)} %reorder.1), calls=%async_computation.2 | async-start | bytes 5242880 | tf_op jit(solution)/shard_map/all_to_all | solution.py:519
  96.8 6.3 %copy.20 = bf16[2048,2,768]{2,0,1:T(8,128)(2,1)} copy(bf16[2048,2,768]{2,1,0:T(2,128)(2,1)} %param.22) | data formatting | bytes 12582912 | tf_op args[8]
  103.1 3.4 %collective-permute-done.8 = bf16[256,512]{1,0:T(8,128)(2,1)S(1)} collective-permute-done((bf16[256,512]{1,0:T(8,128)(2,1)S(1)}, bf16[256,512]{1,0:T(8,128)(2,1)S(1)}, u32[]{:S(2)}, u32[]{:S(2)}) %collective-permute-start.8) | collective-permute-done | bytes 262176 | tf_op jit(solution)/shard_map/ppermute | solution.py:26
  107.9 3.2 %collective-permute-start.15 = (bf16[256,512]{1,0:T(8,128)(2,1)S(1)}, bf16[256,512]{1,0:T(8,128)(2,1)}, u32[]{:S(2)}, u32[]{:S(2)}) collective-permute-start(bf16[256,512]{1,0:T(8,128)(2,1)S(1)} %get-tuple-element.40.o1), channel_id=1, source_target_pairs={{0,3},{1,0},{2,1},{3,2},{4,7},{5,4},{6,5},{7,6},{8,11},{9,8},{10,9... | collective-permute-start | bytes 786440 | tf_op jit(solution)/shard_map/ppermute | solution.py:26
  111.1 3.2 %collective-permute-start.14 = (bf16[256,512]{1,0:T(8,128)(2,1)S(1)}, bf16[256,512]{1,0:T(8,128)(2,1)}, u32[]{:S(2)}, u32[]{:S(2)}) collective-permute-start(bf16[256,512]{1,0:T(8,128)(2,1)S(1)} %get-tuple-element.39.o0), channel_id=1, source_target_pairs={{0,3},{1,0},{2,1},{3,2},{4,7},{5,4},{6,5},{7,6},{8,11},{9,8},{10,9... | collective-permute-start | bytes 786440 | tf_op jit(solution)/shard_map/ppermute | solution.py:26
  114.4 3.9 %collective-permute-done.12.l0 = bf16[256,512]{1,0:T(8,128)(2,1)S(1)} collective-permute-done((bf16[256,512]{1,0:T(8,128)(2,1)S(1)}, bf16[256,512]{1,0:T(8,128)(2,1)S(1)}, u32[]{:S(2)}, u32[]{:S(2)}) %collective-permute-start.12) | collective-permute-done | bytes 262176 | tf_op jit(solution)/shard_map/ppermute | solution.py:26
  118.3 3.3 %collective-permute-start.17 = (bf16[256,512]{1,0:T(8,128)(2,1)}, bf16[256,512]{1,0:T(8,128)(2,1)}, u32[]{:S(2)}, u32[]{:S(2)}) collective-permute-start(bf16[256,512]{1,0:T(8,128)(2,1)} %collective-permute-done.15.r1), channel_id=1, source_target_pairs={{0,3},{1,0},{2,1},{3,2},{4,7},{5,4},{6,5},{7,6},{8,11},{9,8},{10,9... | collective-permute-start | bytes 786440 | tf_op jit(solution)/shard_map/ppermute | solution.py:26
  124.0 4.1 %collective-permute-done.16.f0 = bf16[256,512]{1,0:T(8,128)(2,1)} collective-permute-done((bf16[256,512]{1,0:T(8,128)(2,1)S(1)}, bf16[256,512]{1,0:T(8,128)(2,1)}, u32[]{:S(2)}, u32[]{:S(2)}) %collective-permute-start.16) | collective-permute-done | bytes 262176 | tf_op jit(solution)/shard_map/ppermute | solution.py:26
  128.1 11.0 %feed_forward.1 = (bf16[256,512]{1,0:T(8,128)(2,1)}, bf16[256,512]{1,0:T(8,128)(2,1)}, bf16[256,512]{1,0:T(8,128)(2,1)}, bf16[256,512]{1,0:T(8,128)(2,1)}, bf16[...) custom-call(bf16[256,512]{1,0:T(8,128)(2,1)} %copy-done, ...), custom_call_target="tpu_custom_call" | custom-call | tf_op jit(solution)/shard_map/feed_forward/pallas_call | solution.py:262
  139.2 3.0 %collective-permute-start.22 = (bf16[256,512]{1,0:T(8,128)(2,1)}, bf16[256,512]{1,0:T(8,128)(2,1)S(1)}, u32[]{:S(2)}, u32[]{:S(2)}) collective-permute-start(bf16[256,512]{1,0:T(8,128)(2,1)} %get-tuple-element.49), channel_id=1, source_target_pairs={{0,3},{1,0},{2,1},{3,2},{4,7},{5,4},{6,5},{7,6},{8,11},{9,8},{10,9... | collective-permute-start | bytes 786440 | tf_op jit(solution)/shard_map/ppermute | solution.py:26
  142.2 4.3 %collective-permute-done.22 = bf16[256,512]{1,0:T(8,128)(2,1)S(1)} collective-permute-done((bf16[256,512]{1,0:T(8,128)(2,1)}, bf16[256,512]{1,0:T(8,128)(2,1)S(1)}, u32[]{:S(2)}, u32[]{:S(2)}) %collective-permute-start.22) | collective-permute-done | bytes 262176 | tf_op jit(solution)/shard_map/ppermute | solution.py:26
  148.2 3.6 %collective-permute-start.23 = (bf16[256,512]{1,0:T(8,128)(2,1)}, bf16[256,512]{1,0:T(8,128)(2,1)}, u32[]{:S(2)}, u32[]{:S(2)}) collective-permute-start(bf16[256,512]{1,0:T(8,128)(2,1)} %add_convert_fusion.1), channel_id=1, source_target_pairs={{0,3},{1,0},{2,1},{3,2},{4,7},{5,4},{6,5},{7,6},{8,11},{9,8},{10,9... | collective-permute-start | bytes 786440 | tf_op jit(solution)/shard_map/ppermute | solution.py:26
  152.6 1.7 %add_convert_fusion.3 = bf16[256,512]{1,0:T(8,128)(2,1)} fusion(bf16[256,512]{1,0:T(8,128)(2,1)S(1)} %collective-permute-done.19, bf16[256,512]{1,0:T(8,128)(2,1)} %get-tuple-element.44), kind=kLoop, calls=%fused_computation.5 | loop fusion | flops 524288 | bytes 786432 | tf_op jit(solution)/shard_map/convert_element_type | solution.py:46
  156.4 1.7 %collective-permute-done.23 = bf16[256,512]{1,0:T(8,128)(2,1)} collective-permute-done((bf16[256,512]{1,0:T(8,128)(2,1)}, bf16[256,512]{1,0:T(8,128)(2,1)}, u32[]{:S(2)}, u32[]{:S(2)}) %collective-permute-start.23) | collective-permute-done | bytes 262176 | tf_op jit(solution)/shard_map/ppermute | solution.py:26
  164.3 7.4 %pages.1 = bf16[1,12,256,2,256]{4,3,2,1,0:T(2,128)(2,1)} custom-call(s32[32]{0:T(128)} %slot_map.5, s32[32]{0:T(128)} %prior_len.1, s32[192]{0:T(256)} %reshape.56.table, bf16[32,48,2,256]{3,2,1,0:T(2,128)(2,1)} %all-to-all-done.1.mixed, bf16[32,80,2,256]{3,2,1,0:T(2,128)(2,1)S(1)} %all-to-all-done.2.rest), custom_call_target="tpu_custom_call" | custom-call | tf_op jit(solution)/shard_map/pages/pallas_call | solution.py:487
  (94 shorter events, 23.0 us)
Async XLA Ops:
  0.7 22.2 %copy-start.16 = (f32[2048]{0:T(1024)S(1)}, f32[2048]{0:T(1024)}, u32[]{:S(2)}) copy-start(f32[2048]{0:T(1024)} %param.15) | copy-start | bytes 24580
  0.7 22.8 %copy-start.17 = (f32[2048]{0:T(1024)S(1)}, f32[2048]{0:T(1024)}, u32[]{:S(2)}) copy-start(f32[2048]{0:T(1024)} %param.16) | copy-start | bytes 24580
  0.7 38.6 %all-to-all-start = ((bf16[32,32,2,512]{3,2,1,0:T(2,128)(2,1)}), bf16[32,32,2,512]{3,2,1,0:T(2,128)(2,1)S(1)}, u32[]{:S(2)}, u32[]{:S(2)}) async-start(bf16[32,32,2,512]{3,2,1,0:T(2,128)(2,1)} %bitcast.8), calls=%async_computation | async-start | bytes 4194304 | tf_op jit(solution)/shard_map/all_to_all | solution.py:519
  9.2 10.5 %collective-permute-start = (bf16[256,512]{1,0:T(8,128)(2,1)S(1)}, bf16[256,512]{1,0:T(8,128)(2,1)S(1)}, u32[]{:S(2)}, u32[]{:S(2)}) collective-permute-start(bf16[256,512]{1,0:T(8,128)(2,1)S(1)} %get-tuple-element.53.o0), channel_id=1, source_target_pairs={{0,1},{1,2},{2,3},{3,0},{4,5},{5,6},{6,7},{7,4},{8,9},{9,10},{10,1... | collective-permute-start | bytes 786440 | tf_op jit(solution)/shard_map/ppermute | solution.py:26
  10.8 9.2 %collective-permute-start.3 = (bf16[256,512]{1,0:T(8,128)(2,1)S(1)}, bf16[256,512]{1,0:T(8,128)(2,1)S(1)}, u32[]{:S(2)}, u32[]{:S(2)}) collective-permute-start(bf16[256,512]{1,0:T(8,128)(2,1)S(1)} %get-tuple-element.52.o1), channel_id=1, source_target_pairs={{0,3},{1,0},{2,1},{3,2},{4,7},{5,4},{6,5},{7,6},{8,11},{9,8},{10,9... | collective-permute-start | bytes 786440 | tf_op jit(solution)/shard_map/ppermute | solution.py:26
  12.5 13.5 %collective-permute-start.1 = (bf16[256,512]{1,0:T(8,128)(2,1)S(1)}, bf16[256,512]{1,0:T(8,128)(2,1)S(1)}, u32[]{:S(2)}, u32[]{:S(2)}) collective-permute-start(bf16[256,512]{1,0:T(8,128)(2,1)S(1)} %get-tuple-element.52.o1), channel_id=1, source_target_pairs={{0,1},{1,2},{2,3},{3,0},{4,5},{5,6},{6,7},{7,4},{8,9},{9,10},{10,1... | collective-permute-start | bytes 786440 | tf_op jit(solution)/shard_map/ppermute | solution.py:26
  12.8 13.1 %collective-permute-start.2 = (bf16[256,512]{1,0:T(8,128)(2,1)S(1)}, bf16[256,512]{1,0:T(8,128)(2,1)}, u32[]{:S(2)}, u32[]{:S(2)}) collective-permute-start(bf16[256,512]{1,0:T(8,128)(2,1)S(1)} %get-tuple-element.53.o0), channel_id=1, source_target_pairs={{0,3},{1,0},{2,1},{3,2},{4,7},{5,4},{6,5},{7,6},{8,11},{9,8},{10,9... | collective-permute-start | bytes 786440 | tf_op jit(solution)/shard_map/ppermute | solution.py:26
  19.6 10.7 %collective-permute-start.4 = (bf16[256,512]{1,0:T(8,128)(2,1)S(1)}, bf16[256,512]{1,0:T(8,128)(2,1)}, u32[]{:S(2)}, u32[]{:S(2)}) collective-permute-start(bf16[256,512]{1,0:T(8,128)(2,1)S(1)} %collective-permute-done.l0), channel_id=1, source_target_pairs={{0,1},{1,2},{2,3},{3,0},{4,5},{5,6},{6,7},{7,4},{8,9},{9,10},{10,1... | collective-permute-start | bytes 786440 | tf_op jit(solution)/shard_map/ppermute | solution.py:26
  20.0 10.4 %collective-permute-start.5 = (bf16[256,512]{1,0:T(8,128)(2,1)S(1)}, bf16[256,512]{1,0:T(8,128)(2,1)}, u32[]{:S(2)}, u32[]{:S(2)}) collective-permute-start(bf16[256,512]{1,0:T(8,128)(2,1)S(1)} %collective-permute-done.3.r1), channel_id=1, source_target_pairs={{0,3},{1,0},{2,1},{3,2},{4,7},{5,4},{6,5},{7,6},{8,11},{9,8},{10,9... | collective-permute-start | bytes 786440 | tf_op jit(solution)/shard_map/ppermute | solution.py:26
  43.6 39.5 %all-to-all-start.1 = ((bf16[32,48,2,256]{3,2,1,0:T(2,128)(2,1)}), bf16[32,48,2,256]{3,2,1,0:T(2,128)(2,1)}, u32[]{:S(2)}, u32[]{:S(2)}) async-start(bf16[32,48,2,256]{3,2,1,0:T(2,128)(2,1)} %mix.1), calls=%async_computation.1 | async-start | bytes 3145728 | tf_op jit(solution)/shard_map/all_to_all | solution.py:519
  67.8 10.1 %collective-permute-start.10 = (bf16[256,512]{1,0:T(8,128)(2,1)}, bf16[256,512]{1,0:T(8,128)(2,1)S(1)}, u32[]{:S(2)}, u32[]{:S(2)}) collective-permute-start(bf16[256,512]{1,0:T(8,128)(2,1)} %get-tuple-element.38), channel_id=1, source_target_pairs={{0,3},{1,0},{2,1},{3,2},{4,7},{5,4},{6,5},{7,6},{8,11},{9,8},{10,9... | collective-permute-start | bytes 786440 | tf_op jit(solution)/shard_map/ppermute | solution.py:26
  70.8 24.6 %collective-permute-start.7 = (bf16[256,512]{1,0:T(8,128)(2,1)}, bf16[256,512]{1,0:T(8,128)(2,1)}, u32[]{:S(2)}, u32[]{:S(2)}) collective-permute-start(bf16[256,512]{1,0:T(8,128)(2,1)} %get-tuple-element.34), channel_id=1, source_target_pairs={{0,1},{1,2},{2,3},{3,0},{4,5},{5,6},{6,7},{7,4},{8,9},{9,10},{10,1... | collective-permute-start | bytes 786440 | tf_op jit(solution)/shard_map/ppermute | solution.py:26
  70.8 32.2 %collective-permute-start.9 = (bf16[256,512]{1,0:T(8,128)(2,1)}, bf16[256,512]{1,0:T(8,128)(2,1)S(1)}, u32[]{:S(2)}, u32[]{:S(2)}) collective-permute-start(bf16[256,512]{1,0:T(8,128)(2,1)} %get-tuple-element.36), channel_id=1, source_target_pairs={{0,1},{1,2},{2,3},{3,0},{4,5},{5,6},{6,7},{7,4},{8,9},{9,10},{10,1... | collective-permute-start | bytes 786440 | tf_op jit(solution)/shard_map/ppermute | solution.py:26
  71.4 31.6 %collective-permute-start.6 = (bf16[256,512]{1,0:T(8,128)(2,1)}, bf16[256,512]{1,0:T(8,128)(2,1)S(1)}, u32[]{:S(2)}, u32[]{:S(2)}) collective-permute-start(bf16[256,512]{1,0:T(8,128)(2,1)} %get-tuple-element.32), channel_id=1, source_target_pairs={{0,3},{1,0},{2,1},{3,2},{4,7},{5,4},{6,5},{7,6},{8,11},{9,8},{10,9... | collective-permute-start | bytes 786440 | tf_op jit(solution)/shard_map/ppermute | solution.py:26
  79.6 23.5 %collective-permute-start.11 = (bf16[256,512]{1,0:T(8,128)(2,1)}, bf16[256,512]{1,0:T(8,128)(2,1)}, u32[]{:S(2)}, u32[]{:S(2)}) collective-permute-start(bf16[256,512]{1,0:T(8,128)(2,1)} %add_convert_fusion.5), channel_id=1, source_target_pairs={{0,3},{1,0},{2,1},{3,2},{4,7},{5,4},{6,5},{7,6},{8,11},{9,8},{10,9... | collective-permute-start | bytes 786440 | tf_op jit(solution)/shard_map/ppermute | solution.py:26
  88.1 76.1 %all-to-all-start.2 = ((bf16[32,80,2,256]{3,2,1,0:T(2,128)(2,1)}), bf16[32,80,2,256]{3,2,1,0:T(2,128)(2,1)S(1)}, u32[]{:S(2)}, u32[]{:S(2)}) async-start(bf16[32,80,2,256]{3,2,1,0:T(2,128)(2,1)} %reorder.1), calls=%async_computation.2 | async-start | bytes 5242880 | tf_op jit(solution)/shard_map/all_to_all | solution.py:519
  96.5 10.0 %collective-permute-start.8 = (bf16[256,512]{1,0:T(8,128)(2,1)S(1)}, bf16[256,512]{1,0:T(8,128)(2,1)S(1)}, u32[]{:S(2)}, u32[]{:S(2)}) collective-permute-start(bf16[256,512]{1,0:T(8,128)(2,1)S(1)} %add_convert_fusion.7), channel_id=1, source_target_pairs={{0,1},{1,2},{2,3},{3,0},{4,5},{5,6},{6,7},{7,4},{8,9},{9,10},{10,1... | collective-permute-start | bytes 786440 | tf_op jit(solution)/shard_map/ppermute | solution.py:26
  107.8 10.5 %collective-permute-start.12 = (bf16[256,512]{1,0:T(8,128)(2,1)S(1)}, bf16[256,512]{1,0:T(8,128)(2,1)S(1)}, u32[]{:S(2)}, u32[]{:S(2)}) collective-permute-start(bf16[256,512]{1,0:T(8,128)(2,1)S(1)} %get-tuple-element.39.o0), channel_id=1, source_target_pairs={{0,1},{1,2},{2,3},{3,0},{4,5},{5,6},{6,7},{7,4},{8,9},{9,10},{10,1... | collective-permute-start | bytes 786440 | tf_op jit(solution)/shard_map/ppermute | solution.py:26
  107.9 10.4 %collective-permute-start.15 = (bf16[256,512]{1,0:T(8,128)(2,1)S(1)}, bf16[256,512]{1,0:T(8,128)(2,1)}, u32[]{:S(2)}, u32[]{:S(2)}) collective-permute-start(bf16[256,512]{1,0:T(8,128)(2,1)S(1)} %get-tuple-element.40.o1), channel_id=1, source_target_pairs={{0,3},{1,0},{2,1},{3,2},{4,7},{5,4},{6,5},{7,6},{8,11},{9,8},{10,9... | collective-permute-start | bytes 786440 | tf_op jit(solution)/shard_map/ppermute | solution.py:26
  111.1 12.9 %collective-permute-start.13 = (bf16[256,512]{1,0:T(8,128)(2,1)S(1)}, bf16[256,512]{1,0:T(8,128)(2,1)}, u32[]{:S(2)}, u32[]{:S(2)}) collective-permute-start(bf16[256,512]{1,0:T(8,128)(2,1)S(1)} %get-tuple-element.40.o1), channel_id=1, source_target_pairs={{0,1},{1,2},{2,3},{3,0},{4,5},{5,6},{6,7},{7,4},{8,9},{9,10},{10,1... | collective-permute-start | bytes 786440 | tf_op jit(solution)/shard_map/ppermute | solution.py:26
  111.1 12.9 %collective-permute-start.14 = (bf16[256,512]{1,0:T(8,128)(2,1)S(1)}, bf16[256,512]{1,0:T(8,128)(2,1)}, u32[]{:S(2)}, u32[]{:S(2)}) collective-permute-start(bf16[256,512]{1,0:T(8,128)(2,1)S(1)} %get-tuple-element.39.o0), channel_id=1, source_target_pairs={{0,3},{1,0},{2,1},{3,2},{4,7},{5,4},{6,5},{7,6},{8,11},{9,8},{10,9... | collective-permute-start | bytes 786440 | tf_op jit(solution)/shard_map/ppermute | solution.py:26
  118.3 9.8 %collective-permute-start.16 = (bf16[256,512]{1,0:T(8,128)(2,1)S(1)}, bf16[256,512]{1,0:T(8,128)(2,1)}, u32[]{:S(2)}, u32[]{:S(2)}) collective-permute-start(bf16[256,512]{1,0:T(8,128)(2,1)S(1)} %collective-permute-done.12.l0), channel_id=1, source_target_pairs={{0,1},{1,2},{2,3},{3,0},{4,5},{5,6},{6,7},{7,4},{8,9},{9,10},{10,1... | collective-permute-start | bytes 786440 | tf_op jit(solution)/shard_map/ppermute | solution.py:26
  118.3 9.8 %collective-permute-start.17 = (bf16[256,512]{1,0:T(8,128)(2,1)}, bf16[256,512]{1,0:T(8,128)(2,1)}, u32[]{:S(2)}, u32[]{:S(2)}) collective-permute-start(bf16[256,512]{1,0:T(8,128)(2,1)} %collective-permute-done.15.r1), channel_id=1, source_target_pairs={{0,3},{1,0},{2,1},{3,2},{4,7},{5,4},{6,5},{7,6},{8,11},{9,8},{10,9... | collective-permute-start | bytes 786440 | tf_op jit(solution)/shard_map/ppermute | solution.py:26
  122.8 32.7 %copy-start.20 = (s32[32,6]{0,1:T(8,128)S(1)}, s32[32,6]{0,1:T(8,128)}, u32[]{:S(2)}) copy-start(s32[32,6]{0,1:T(8,128)} %param.27) | copy-start | bytes 2308
  139.2 23.1 %copy-start.1 = (bf16[256,512]{1,0:T(8,128)(2,1)S(1)}, bf16[256,512]{1,0:T(8,128)(2,1)}, u32[]{:S(2)}) copy-start(bf16[256,512]{1,0:T(8,128)(2,1)} %copy-done) | copy-start | bytes 786436
  139.2 23.1 %copy-start.9 = (bf16[256,512]{1,0:T(8,128)(2,1)S(1)}, bf16[256,512]{1,0:T(8,128)(2,1)}, u32[]{:S(2)}) copy-start(bf16[256,512]{1,0:T(8,128)(2,1)} %get-tuple-element.42) | copy-start | bytes 786436
  139.2 7.3 %collective-permute-start.22 = (bf16[256,512]{1,0:T(8,128)(2,1)}, bf16[256,512]{1,0:T(8,128)(2,1)S(1)}, u32[]{:S(2)}, u32[]{:S(2)}) collective-permute-start(bf16[256,512]{1,0:T(8,128)(2,1)} %get-tuple-element.49), channel_id=1, source_target_pairs={{0,3},{1,0},{2,1},{3,2},{4,7},{5,4},{6,5},{7,6},{8,11},{9,8},{10,9... | collective-permute-start | bytes 786440 | tf_op jit(solution)/shard_map/ppermute | solution.py:26
  142.2 10.4 %collective-permute-start.19 = (bf16[256,512]{1,0:T(8,128)(2,1)}, bf16[256,512]{1,0:T(8,128)(2,1)S(1)}, u32[]{:S(2)}, u32[]{:S(2)}) collective-permute-start(bf16[256,512]{1,0:T(8,128)(2,1)} %get-tuple-element.45), channel_id=1, source_target_pairs={{0,1},{1,2},{2,3},{3,0},{4,5},{5,6},{6,7},{7,4},{8,9},{9,10},{10,1... | collective-permute-start | bytes 786440 | tf_op jit(solution)/shard_map/ppermute | solution.py:26
  142.2 14.2 %collective-permute-start.21 = (bf16[256,512]{1,0:T(8,128)(2,1)}, bf16[256,512]{1,0:T(8,128)(2,1)S(1)}, u32[]{:S(2)}, u32[]{:S(2)}) collective-permute-start(bf16[256,512]{1,0:T(8,128)(2,1)} %get-tuple-element.47), channel_id=1, source_target_pairs={{0,1},{1,2},{2,3},{3,0},{4,5},{5,6},{6,7},{7,4},{8,9},{9,10},{10,1... | collective-permute-start | bytes 786440 | tf_op jit(solution)/shard_map/ppermute | solution.py:26
  148.2 9.9 %collective-permute-start.23 = (bf16[256,512]{1,0:T(8,128)(2,1)}, bf16[256,512]{1,0:T(8,128)(2,1)}, u32[]{:S(2)}, u32[]{:S(2)}) collective-permute-start(bf16[256,512]{1,0:T(8,128)(2,1)} %add_convert_fusion.1), channel_id=1, source_target_pairs={{0,3},{1,0},{2,1},{3,2},{4,7},{5,4},{6,5},{7,6},{8,11},{9,8},{10,9... | collective-permute-start | bytes 786440 | tf_op jit(solution)/shard_map/ppermute | solution.py:26
  151.8 9.1 %collective-permute-start.18 = (bf16[256,512]{1,0:T(8,128)(2,1)}, bf16[256,512]{1,0:T(8,128)(2,1)}, u32[]{:S(2)}, u32[]{:S(2)}) collective-permute-start(bf16[256,512]{1,0:T(8,128)(2,1)} %get-tuple-element.43), channel_id=1, source_target_pairs={{0,3},{1,0},{2,1},{3,2},{4,7},{5,4},{6,5},{7,6},{8,11},{9,8},{10,9... | collective-permute-start | bytes 786440 | tf_op jit(solution)/shard_map/ppermute | solution.py:26
  154.4 7.9 %collective-permute-start.20 = (bf16[256,512]{1,0:T(8,128)(2,1)}, bf16[256,512]{1,0:T(8,128)(2,1)}, u32[]{:S(2)}, u32[]{:S(2)}) collective-permute-start(bf16[256,512]{1,0:T(8,128)(2,1)} %add_convert_fusion.3), channel_id=1, source_target_pairs={{0,1},{1,2},{2,3},{3,0},{4,5},{5,6},{6,7},{7,4},{8,9},{9,10},{10,1... | collective-permute-start | bytes 786440 | tf_op jit(solution)/shard_map/ppermute | solution.py:26
  (17 other events, 220.4 us)
